TPU v7x, 512 devices: a whole 4x8x8 slice. The times are simulated.
512 devices in a mesh: sec: 128 (over y, z, core), ch: 4 (over x).
Axes of the slice: x: 4, y: 8, z: 8, core: 2. Of those that a mesh axis runs over, the one named last changes fastest.
Arguments:
- outer_wave: float32 [2, 1536, 16384], P(None, 'ch', 'sec'), may hold values from -3 to 3
- inner_wave: float32 [2, 32768], P(None, ('sec', 'ch'))
- surface: float32 [2, 32768, 1536], P(None, ('sec', 'ch'))
- energies: float32 [32768], P(('sec', 'ch')), may hold values from -2 to 100
- coefficients: float32 [12, 8, 128, 128], P('ch'), as said below
- block_cols: int32 [12, 8], replicated, may hold values from 0 to 11, as said below
- block_kind: int32 [12, 8], replicated, may hold values from 0 to 2, as said below
- polarisation: int32 [12, 8], replicated, may hold values from 0 to 2, as said below
- laser_field: float32 [3], replicated, may hold values from -0.05 to 0.05
Outputs:
- new_outer: float32 [2, 1536, 16384], P(None, 'ch', 'sec')
- new_inner: float32 [2, 32768], P(None, ('sec', 'ch'))
Inputs may be any that keep to these rules, and one draw needn't show every extreme that they name: Each row of block_cols names 8 different channel blocks; block c stands in row b exactly when b stands in row c, and the two slots then carry the same kind, the same polarisation and mutually transposed coefficient blocks. `block_kind`: equal for the two slots of a mutually coupled pair of blocks. `polarisation`: equal for the two slots of a mutually coupled pair of blocks. coefficients of the slot that couples block c to block b are the transpose of those that couple b to c; a block coupled to itself has a symmetric block.
All inputs are finite; a program needn't handle non-finite values.
Results may differ from a plain program's by a relative error of at most 0.0003.
Values sent between devices are 32-bit elements; how exact they have to be, the bound alone decides.
A program may use at most 64 MiB of HBM per device.

v0:
```python
import jax
import jax.numpy as jnp
from jax import lax
from jax.sharding import PartitionSpec as P

ITERS = 4


inner_radius = 20.0
grid_step = 0.08
time_step = 0.01
stencil_scale = 1.0 / (24.0 * grid_step * grid_step)
taylor_terms = 10
squarings = 7
highest = lax.Precision.HIGHEST


def with_halo(x, sides, width):
    for axis, dim in sides:
        size, length = (lax.axis_size(axis), x.shape[dim])
        up = [(i, (i + 1) % size) for i in range(size - 1)]
        down = [(j, i) for i, j in up]
        last = lax.slice_in_dim(x, length - width, length, axis=dim)
        initial = lax.slice_in_dim(x, 0, width, axis=dim)
        before = lax.ppermute(last, axis, up)
        after = lax.ppermute(initial, axis, down)
        x = jnp.concatenate([before, x, after], axis=dim)
    return x


def radial_factor(kind_map, polar_map, laser_field, radius):
    radius_ratio = inner_radius / radius
    dipole_like = radius_ratio * radius_ratio
    quadrupole_like = dipole_like * radius_ratio
    chosen = jnp.sum(
        jnp.where(polar_map[..., None] == jnp.arange(3, dtype=jnp.int32), laser_field, 0.0), axis=-1
    )
    laser_term = chosen[..., None] * radius
    kind_wide = kind_map[..., None]
    return jnp.where(
        kind_wide == 0, dipole_like, jnp.where(kind_wide == 1, quadrupole_like, laser_term)
    )


def kinetic(padded):
    return stencil_scale * (
        padded[:, :, :-4]
        - 16.0 * padded[:, :, 1:-3]
        + 30.0 * padded[:, :, 2:-2]
        - 16.0 * padded[:, :, 3:-1]
        + padded[:, :, 4:]
    )


def complex_scale(scale_real, scale_imag, vector):
    return jnp.stack(
        [
            scale_real * vector[0] - scale_imag * vector[1],
            scale_real * vector[1] + scale_imag * vector[0],
        ]
    )


def propagate(hess_real, hess_imag):
    top_half = jnp.concatenate([time_step * hess_imag, time_step * hess_real], axis=1)
    bottom_half = jnp.concatenate([-time_step * hess_real, time_step * hess_imag], axis=1)
    scaled_block = jnp.concatenate([top_half, bottom_half], axis=0) / 2.0**squarings
    identity = jnp.eye(2 * ITERS, dtype=jnp.float32)
    series = identity
    for degree in range(taylor_terms, 0, -1):
        series = identity + jnp.dot(scaled_block, series, precision=highest) / degree
    for repeat in range(squarings):
        series = jnp.dot(series, series, precision=highest)
    return (series[:ITERS, 0], series[ITERS:, 0])


def per_device(
    outer_wave,
    inner_wave,
    surface,
    energies,
    coefficients,
    block_cols,
    block_kind,
    polarisation,
    laser_field,
):
    sec_index = lax.axis_index("sec")
    ch_index = lax.axis_index("ch")
    ch_count = lax.axis_size("ch")
    ch_dev = outer_wave.shape[1]
    rad_dev = outer_wave.shape[2]
    block_size = coefficients.shape[2]
    rows_dev = coefficients.shape[0]
    positions = sec_index * rad_dev + jnp.arange(rad_dev, dtype=jnp.int32)
    radius = inner_radius + (positions + 1).astype(jnp.float32) * grid_step
    first_sector = (sec_index == 0).astype(jnp.float32)
    local_cols = lax.dynamic_slice_in_dim(block_cols, ch_index * rows_dev, rows_dev, 0)
    local_kind = lax.dynamic_slice_in_dim(block_kind, ch_index * rows_dev, rows_dev, 0)
    local_polar = lax.dynamic_slice_in_dim(polarisation, ch_index * rows_dev, rows_dev, 0)
    local_factor = radial_factor(local_kind, local_polar, laser_field, radius)
    local_sq = jnp.sum(outer_wave * outer_wave) + jnp.sum(inner_wave * inner_wave)
    start_sq = lax.psum(local_sq, ("sec", "ch"))
    start_norm = jnp.sqrt(start_sq + 1e-06)
    basis_outer = [outer_wave / start_norm]
    basis_inner = [inner_wave / start_norm]
    hess_real = jnp.zeros((ITERS, ITERS), jnp.float32)
    hess_imag = jnp.zeros((ITERS, ITERS), jnp.float32)
    for column in range(ITERS):
        boundary_outer = basis_outer[column]
        partial_sum = jnp.einsum("xk,lkc->xlc", basis_inner[column], surface, precision=highest)
        edge_pair = (
            jnp.stack([boundary_outer[:, :, 0], boundary_outer[:, :, 1]], axis=1) * first_sector
        )
        edge_blank = jnp.zeros((2, 2, ch_dev * ch_count), jnp.float32)
        edge_full = lax.dynamic_update_slice_in_dim(edge_blank, edge_pair, ch_index * ch_dev, 2)
        whole_sum, boundary_edge_all = lax.psum((partial_sum, edge_full), ("sec", "ch"))
        ghosts = lax.dynamic_slice_in_dim(whole_sum, ch_index * ch_dev, ch_dev, 2)
        outer = basis_outer[column]
        rim_values = jnp.stack([ghosts[:, 1], ghosts[:, 0]], axis=2) * first_sector
        padded = with_halo(outer, (("sec", 2),), 2)
        padded = padded.at[:, :, 0:2].add(rim_values)
        full_rows = lax.all_gather(outer, "ch", axis=1, tiled=True)
        grouped = full_rows.reshape(2, -1, block_size, rad_dev)
        picked = jnp.take(grouped, local_cols, axis=1)
        product = jnp.einsum("lsab,xlsbr->xlsar", coefficients, picked, precision=highest)
        outer_image = kinetic(padded) + jnp.sum(
            product * local_factor[None, :, :, None, :], axis=2
        ).reshape(2, ch_dev, rad_dev)
        mixed_edge = -16.0 * boundary_edge_all[:, 0] + boundary_edge_all[:, 1]
        inner_image = energies * basis_inner[column] + stencil_scale * (
            jnp.einsum("xc,kc->xk", mixed_edge, surface[0], precision=highest)
            + jnp.einsum("xc,kc->xk", boundary_edge_all[:, 0], surface[1], precision=highest)
        )
        w_outer = outer_image
        w_inner = inner_image
        reals = []
        imags = []
        for vec_outer, vec_inner in zip(basis_outer, basis_inner):
            reals.append(jnp.sum(vec_outer * w_outer) + jnp.sum(vec_inner * w_inner))
            imags.append(
                jnp.sum(vec_outer[0] * w_outer[1] - vec_outer[1] * w_outer[0])
                + jnp.sum(vec_inner[0] * w_inner[1] - vec_inner[1] * w_inner[0])
            )
        loc_real = jnp.stack(reals)
        loc_imag = jnp.stack(imags)
        proj_real, proj_imag = lax.psum((loc_real, loc_imag), ("sec", "ch"))
        for row_index in range(column + 1):
            w_outer = w_outer - complex_scale(
                proj_real[row_index], proj_imag[row_index], basis_outer[row_index]
            )
            w_inner = w_inner - complex_scale(
                proj_real[row_index], proj_imag[row_index], basis_inner[row_index]
            )
        hess_real = hess_real.at[: column + 1, column].set(proj_real)
        hess_imag = hess_imag.at[: column + 1, column].set(proj_imag)
        if column + 1 < ITERS:
            norm_sq = lax.psum(
                jnp.sum(w_outer * w_outer) + jnp.sum(w_inner * w_inner), ("sec", "ch")
            )
            next_norm = jnp.sqrt(norm_sq + 1e-06)
            hess_real = hess_real.at[column + 1, column].set(next_norm)
            basis_outer.append(w_outer / next_norm)
            basis_inner.append(w_inner / next_norm)
    coef_real, coef_imag = propagate(hess_real, hess_imag)
    accum_outer = jnp.zeros_like(outer_wave)
    accum_inner = jnp.zeros_like(inner_wave)
    for column in range(ITERS):
        accum_outer = accum_outer + complex_scale(
            coef_real[column], coef_imag[column], basis_outer[column]
        )
        accum_inner = accum_inner + complex_scale(
            coef_real[column], coef_imag[column], basis_inner[column]
        )
    return (accum_outer * start_norm, accum_inner * start_norm)


def solution(mesh):
    placed = (
        P(None, "ch", "sec"),
        P(None, ("sec", "ch")),
        P(None, ("sec", "ch"), None),
        P(("sec", "ch")),
        P("ch", None, None, None),
        P(),
        P(),
        P(),
        P(),
    )
    return jax.shard_map(
        per_device,
        mesh=mesh,
        in_specs=placed,
        out_specs=(P(None, "ch", "sec"), P(None, ("sec", "ch"))),
        check_vma=False,
    )
```

profile of v0, /device:TPU:1, one launch (start us, length us, event | category | flops | bytes accessed | tf_op | source)
XLA Modules:
  0.0 1477.4 jit_solution(9369431426604084190)
XLA Ops:
  11.7 106.1 %psum.140 = f32[]{:T(128)} all-reduce(f32[]{:T(128)S(6)} %add.435), channel_id=1, replica_groups=mesh['sec'=128,'ch'=4] {'sec','ch'}, use_global_device_ids=true, to_apply=%region_2.3 | all-reduce | flops 1 | bytes 8 | tf_op jit(solution)/shard_map/psum | solution.py:103
  125.1 3.0 collective-permute-start
  130.9 96.9 %all-reduce.9 = (f32[2,2,1536]{2,0,1:T(2,128)S(1)}, f32[2,2,1536]{2,0,1:T(2,128)S(1)}) all-reduce(f32[2,2,1536]{2,0,1:T(2,128)S(1)} %fusion.151, f32[2,2,1536]{2,0,1:T(2,128)S(1)} %fusion.121), channel_id=1, replica_groups=mesh['sec'=128,'ch'=4] {'sec','ch'}, use_global_device_ids=true, to_apply=%region_3.4 | all-reduce | flops 12288 | bytes 98304 | tf_op jit(solution)/shard_map/psum | solution.py:117
  237.4 4.2 gather_fusion
  241.7 3.6 copy.380
  245.2 4.8 multiply_reduce_fusion.3
  251.0 3.6 multiply_reduce_fusion.16
  257.9 96.5 %all-reduce.8 = (f32[1]{0:T(128)}, f32[1]{0:T(128)}) all-reduce(f32[1]{0:T(128)} %bitcast.14, f32[1]{0:T(128)} %bitcast.16), channel_id=1, replica_groups=mesh['sec'=128,'ch'=4] {'sec','ch'}, use_global_device_ids=true, to_apply=%region_9.11 | all-reduce | flops 2 | bytes 16 | tf_op jit(solution)/shard_map/psum | solution.py:147
  360.5 94.9 %psum.145 = f32[]{:T(128)} all-reduce(f32[]{:T(128)S(6)} %add.456), channel_id=1, replica_groups=mesh['sec'=128,'ch'=4] {'sec','ch'}, use_global_device_ids=true, to_apply=%region_15.17 | all-reduce | flops 1 | bytes 8 | tf_op jit(solution)/shard_map/psum | solution.py:158
  461.8 3.0 collective-permute-start.2
  469.9 99.9 %all-reduce.7 = (f32[2,2,1536]{2,0,1:T(2,128)}, f32[2,2,1536]{2,0,1:T(2,128)}) all-reduce(f32[2,2,1536]{2,0,1:T(2,128)} %fusion.149, f32[2,2,1536]{2,0,1:T(2,128)} %fusion.122), channel_id=1, replica_groups=mesh['sec'=128,'ch'=4] {'sec','ch'}, use_global_device_ids=true, to_apply=%region_16.18 | all-reduce | flops 12288 | bytes 98304 | tf_op jit(solution)/shard_map/psum | solution.py:117
  584.2 3.9 gather_fusion.1
  588.2 3.6 copy.391
  591.8 5.5 multiply_reduce_fusion.2
  599.2 3.8 multiply_reduce_fusion.14
  609.5 95.0 %all-reduce.6 = (f32[2]{0:T(128)S(1)}, f32[2]{0:T(128)S(1)}) all-reduce(f32[2]{0:T(128)S(1)} %pad_maximum_fusion.4, f32[2]{0:T(128)S(1)} %pad_maximum_fusion.5), channel_id=1, replica_groups=mesh['sec'=128,'ch'=4] {'sec','ch'}, use_global_device_ids=true, to_apply=%region_23.25 | all-reduce | flops 4 | bytes 32 | tf_op jit(solution)/shard_map/psum | solution.py:147
  716.8 95.0 %psum.150 = f32[]{:T(128)} all-reduce(f32[]{:T(128)S(6)} %add.474), channel_id=1, replica_groups=mesh['sec'=128,'ch'=4] {'sec','ch'}, use_global_device_ids=true, to_apply=%region_32.34 | all-reduce | flops 1 | bytes 8 | tf_op jit(solution)/shard_map/psum | solution.py:158
  825.8 3.0 collective-permute-start.4
  833.9 98.1 %all-reduce.5 = (f32[2,2,1536]{2,0,1:T(2,128)}, f32[2,2,1536]{2,0,1:T(2,128)}) all-reduce(f32[2,2,1536]{2,0,1:T(2,128)} %fusion.147, f32[2,2,1536]{2,0,1:T(2,128)} %fusion.123), channel_id=1, replica_groups=mesh['sec'=128,'ch'=4] {'sec','ch'}, use_global_device_ids=true, to_apply=%region_33.35 | all-reduce | flops 12288 | bytes 98304 | tf_op jit(solution)/shard_map/psum | solution.py:117
  948.8 3.9 gather_fusion.2
  952.7 3.6 copy.399
  956.3 5.5 multiply_reduce_fusion.1
  963.8 4.2 multiply_reduce_fusion.11
  980.9 95.7 %all-reduce.4 = (f32[3]{0:T(128)}, f32[3]{0:T(128)}) all-reduce(f32[3]{0:T(128)} %pad_maximum_fusion.6, f32[3]{0:T(128)} %pad_maximum_fusion.7), channel_id=1, replica_groups=mesh['sec'=128,'ch'=4] {'sec','ch'}, use_global_device_ids=true, to_apply=%region_42.44 | all-reduce | flops 6 | bytes 48 | tf_op jit(solution)/shard_map/psum | solution.py:147
  1095.5 94.8 %psum.155 = f32[]{:T(128)} all-reduce(f32[]{:T(128)S(6)} %add.496), channel_id=1, replica_groups=mesh['sec'=128,'ch'=4] {'sec','ch'}, use_global_device_ids=true, to_apply=%region_52.54 | all-reduce | flops 1 | bytes 8 | tf_op jit(solution)/shard_map/psum | solution.py:158
  1197.4 3.0 collective-permute-start.6
  1205.4 99.8 %all-reduce.3 = (f32[2,2,1536]{2,0,1:T(2,128)}, f32[2,2,1536]{2,0,1:T(2,128)}) all-reduce(f32[2,2,1536]{2,0,1:T(2,128)} %fusion.145, f32[2,2,1536]{2,0,1:T(2,128)} %fusion.124), channel_id=1, replica_groups=mesh['sec'=128,'ch'=4] {'sec','ch'}, use_global_device_ids=true, to_apply=%region_53.55 | all-reduce | flops 12288 | bytes 98304 | tf_op jit(solution)/shard_map/psum | solution.py:117
  1326.8 4.2 gather_fusion.3
  1331.0 3.6 copy.407
  1334.6 5.5 multiply_reduce_fusion
  1342.1 4.3 multiply_reduce_fusion.7
  1357.7 94.9 %all-reduce.2 = (f32[4,1]{0,1:T(1,128)S(1)}, f32[4,1]{0,1:T(1,128)S(1)}) all-reduce(f32[4,1]{0,1:T(1,128)S(1)} %maximum_bitcast_fusion, f32[4,1]{0,1:T(1,128)S(1)} %maximum_bitcast_fusion.1), channel_id=1, replica_groups=mesh['sec'=128,'ch'=4] {'sec','ch'}, use_global_device_ids=true, to_apply=%region_64.66 | all-reduce | flops 8 | bytes 64 | tf_op jit(solution)/shard_map/psum | solution.py:147
  (276 shorter events, 181.8 us)
Async XLA Ops:
  7.2 238.1 %copy-start = (f32[3,8,128,128]{3,2,1,0:T(8,128)S(1)}, f32[3,8,128,128]{3,2,1,0:T(8,128)}, u32[]{:S(2)}) copy-start(f32[3,8,128,128]{3,2,1,0:T(8,128)} %param.45) | copy-start | bytes 4718596
  7.2 123.2 %copy-start.38 = (f32[2,64]{1,0:T(2,128)S(1)}, f32[2,64]{1,0:T(2,128)}, u32[]{:S(2)}) copy-start(f32[2,64]{1,0:T(2,128)} %param.42) | copy-start | bytes 1540
  7.2 120.9 %copy-start.36 = (s32[12,8]{0,1:T(8,128)S(1)}, s32[12,8]{0,1:T(8,128)}, u32[]{:S(2)}) copy-start(s32[12,8]{0,1:T(8,128)} %param.46) | copy-start | bytes 1156
  7.2 120.9 %copy-start.37 = (s32[12,8]{0,1:T(8,128)S(1)}, s32[12,8]{0,1:T(8,128)}, u32[]{:S(2)}) copy-start(s32[12,8]{0,1:T(8,128)} %param.47) | copy-start | bytes 1156
  7.2 121.0 %copy-start.35 = (s32[12,8]{0,1:T(8,128)S(1)}, s32[12,8]{0,1:T(8,128)}, u32[]{:S(2)}) copy-start(s32[12,8]{0,1:T(8,128)} %param.48) | copy-start | bytes 1156
  7.2 123.1 %copy-start.3 = (f32[2,64,1536]{2,1,0:T(8,128)S(1)}, f32[2,64,1536]{2,1,0:T(8,128)}, u32[]{:S(2)}) copy-start(f32[2,64,1536]{2,1,0:T(8,128)} %param.43) | copy-start | bytes 2359300
  7.2 221.6 %copy-start.29 = (f32[64]{0:T(128)S(1)}, f32[64]{0:T(128)}, u32[]{:S(2)}) copy-start(f32[64]{0:T(128)} %param.44) | copy-start | bytes 772
  7.2 223.4 %copy-start.39 = (f32[3]{0:T(128)S(1)}, f32[3]{0:T(128)}, u32[]{:S(2)}) copy-start(f32[3]{0:T(128)} %param.49) | copy-start | bytes 40
  7.3 230.2 %all-gather.5.cloned.1.call-start = ((), (), s32[]{:S(2)}) async-start(), calls=%async_computation | async-start | bytes 1966080 | tf_op jit(solution)/shard_map/all_gather | solution.py:123
  120.3 113.5 %copy-start.1 = (f32[2,384,128]{2,1,0:T(8,128)S(1)}, f32[2,384,128]{2,1,0:T(8,128)}, u32[]{:S(2)}) copy-start(f32[2,384,128]{2,1,0:T(8,128)} %broadcast_divide_fusion.3) | copy-start | bytes 1179652
  120.3 464.0 %all-gather.7.cloned.1.call-start = ((), (), s32[]{:S(2)}) async-start(), calls=%async_computation.1 | async-start | bytes 1966080 | tf_op jit(solution)/shard_map/all_gather | solution.py:123
  122.5 111.3 %collective-permute-start.1 = (f32[2,384,2]{2,1,0:T(8,128)}, f32[2,384,2]{2,1,0:T(8,128)}, u32[]{:S(2)}, u32[]{:S(2)}) collective-permute-start(f32[2,384,2]{2,1,0:T(8,128)} %get-tuple-element.291), channel_id=1, source_target_pairs={{4,0},{8,4},{12,8},{16,12},{20,16},{24,20},{28,24},{32,28},{36,32}... | collective-permute-start | bytes 18440 | tf_op jit(solution)/shard_map/ppermute | solution.py:26
  125.1 107.8 %collective-permute-start = (f32[2,384,2]{2,1,0:T(8,128)}, f32[2,384,2]{2,1,0:T(8,128)S(1)}, u32[]{:S(2)}, u32[]{:S(2)}) collective-permute-start(f32[2,384,2]{2,1,0:T(8,128)} %get-tuple-element.290), channel_id=1, source_target_pairs={{0,4},{4,8},{8,12},{12,16},{16,20},{20,24},{24,28},{28,32},{32,36}... | collective-permute-start | bytes 18440 | tf_op jit(solution)/shard_map/ppermute | solution.py:25
  254.6 344.6 %copy-start.6 = (f32[2,384,128]{2,1,0:T(8,128)}, f32[2,384,128]{2,1,0:T(8,128)S(1)}, u32[]{:S(2)}) copy-start(f32[2,384,128]{2,1,0:T(8,128)S(1)} %get-tuple-element.261) | copy-start | bytes 1179652
  355.7 100.3 %copy-start.12 = (f32[1,384,128]{2,1,0:T(8,128)}, f32[1,384,128]{2,1,0:T(8,128)S(1)}, u32[]{:S(2)}) copy-start(f32[1,384,128]{2,1,0:T(8,128)S(1)} %get-tuple-element.288) | copy-start | bytes 589828
  355.7 100.3 %copy-start.13 = (f32[1,384,128]{2,1,0:T(8,128)}, f32[1,384,128]{2,1,0:T(8,128)S(1)}, u32[]{:S(2)}) copy-start(f32[1,384,128]{2,1,0:T(8,128)S(1)} %get-tuple-element.289) | copy-start | bytes 589828
  456.9 122.8 %copy-start.2 = (f32[2,384,128]{2,1,0:T(8,128)S(1)}, f32[2,384,128]{2,1,0:T(8,128)}, u32[]{:S(2)}) copy-start(f32[2,384,128]{2,1,0:T(8,128)} %broadcast_divide_fusion.2) | copy-start | bytes 1179652
  456.9 491.9 %all-gather.9.cloned.1.call-start = ((), (), s32[]{:S(2)}) async-start(), calls=%async_computation.2 | async-start | bytes 1966080 | tf_op jit(solution)/shard_map/all_gather | solution.py:123
  459.2 120.5 %collective-permute-start.3 = (f32[2,384,2]{2,1,0:T(8,128)}, f32[2,384,2]{2,1,0:T(8,128)}, u32[]{:S(2)}, u32[]{:S(2)}) collective-permute-start(f32[2,384,2]{2,1,0:T(8,128)} %get-tuple-element.287), channel_id=1, source_target_pairs={{4,0},{8,4},{12,8},{16,12},{20,16},{24,20},{28,24},{32,28},{36,32}... | collective-permute-start | bytes 18440 | tf_op jit(solution)/shard_map/ppermute | solution.py:26
  461.8 116.0 %collective-permute-start.2 = (f32[2,384,2]{2,1,0:T(8,128)}, f32[2,384,2]{2,1,0:T(8,128)}, u32[]{:S(2)}, u32[]{:S(2)}) collective-permute-start(f32[2,384,2]{2,1,0:T(8,128)} %get-tuple-element.286), channel_id=1, source_target_pairs={{0,4},{4,8},{8,12},{12,16},{16,20},{20,24},{24,28},{28,32},{32,36}... | collective-permute-start | bytes 18440 | tf_op jit(solution)/shard_map/ppermute | solution.py:25
  707.1 105.5 %copy-start.14 = (f32[1,384,128]{2,1,0:T(8,128)}, f32[1,384,128]{2,1,0:T(8,128)S(1)}, u32[]{:S(2)}) copy-start(f32[1,384,128]{2,1,0:T(8,128)S(1)} %get-tuple-element.284) | copy-start | bytes 589828
  707.1 105.5 %copy-start.15 = (f32[1,384,128]{2,1,0:T(8,128)}, f32[1,384,128]{2,1,0:T(8,128)S(1)}, u32[]{:S(2)}) copy-start(f32[1,384,128]{2,1,0:T(8,128)S(1)} %get-tuple-element.285) | copy-start | bytes 589828
  814.6 129.7 %copy-start.4 = (f32[2,384,128]{2,1,0:T(8,128)S(1)}, f32[2,384,128]{2,1,0:T(8,128)}, u32[]{:S(2)}) copy-start(f32[2,384,128]{2,1,0:T(8,128)} %broadcast_divide_fusion.1) | copy-start | bytes 1179652
  814.6 512.2 %all-gather.11.cloned.1.call-start = ((), (), s32[]{:S(2)}) async-start(), calls=%async_computation.3 | async-start | bytes 1966080 | tf_op jit(solution)/shard_map/all_gather | solution.py:123
  823.2 121.0 %collective-permute-start.5 = (f32[2,384,2]{2,1,0:T(8,128)}, f32[2,384,2]{2,1,0:T(8,128)}, u32[]{:S(2)}, u32[]{:S(2)}) collective-permute-start(f32[2,384,2]{2,1,0:T(8,128)} %get-tuple-element.281), channel_id=1, source_target_pairs={{4,0},{8,4},{12,8},{16,12},{20,16},{24,20},{28,24},{32,28},{36,32}... | collective-permute-start | bytes 18440 | tf_op jit(solution)/shard_map/ppermute | solution.py:26
  825.8 116.6 %collective-permute-start.4 = (f32[2,384,2]{2,1,0:T(8,128)}, f32[2,384,2]{2,1,0:T(8,128)}, u32[]{:S(2)}, u32[]{:S(2)}) collective-permute-start(f32[2,384,2]{2,1,0:T(8,128)} %get-tuple-element.280), channel_id=1, source_target_pairs={{0,4},{4,8},{8,12},{12,16},{16,20},{20,24},{24,28},{28,32},{32,36}... | collective-permute-start | bytes 18440 | tf_op jit(solution)/shard_map/ppermute | solution.py:25
  1194.9 128.1 %collective-permute-start.7 = (f32[2,384,2]{2,1,0:T(8,128)}, f32[2,384,2]{2,1,0:T(8,128)}, u32[]{:S(2)}, u32[]{:S(2)}) collective-permute-start(f32[2,384,2]{2,1,0:T(8,128)} %get-tuple-element.273), channel_id=1, source_target_pairs={{4,0},{8,4},{12,8},{16,12},{20,16},{24,20},{28,24},{32,28},{36,32}... | collective-permute-start | bytes 18440 | tf_op jit(solution)/shard_map/ppermute | solution.py:26
  1197.4 123.8 %collective-permute-start.6 = (f32[2,384,2]{2,1,0:T(8,128)}, f32[2,384,2]{2,1,0:T(8,128)}, u32[]{:S(2)}, u32[]{:S(2)}) collective-permute-start(f32[2,384,2]{2,1,0:T(8,128)} %get-tuple-element.272), channel_id=1, source_target_pairs={{0,4},{4,8},{8,12},{12,16},{16,20},{20,24},{24,28},{28,32},{32,36}... | collective-permute-start | bytes 18440 | tf_op jit(solution)/shard_map/ppermute | solution.py:25
  1334.6 7.5 copy-start.7
  1342.1 15.5 %copy-start.26 = (f32[4,4]{0,1:T(4,128)S(1)}, f32[4,4]{0,1:T(4,128)}, u32[]{:S(2)}) copy-start(f32[4,4]{0,1:T(4,128)} %scatter.50) | copy-start | bytes 196
  1346.4 115.7 %copy-start.21 = (f32[2,64]{1,0:T(2,128)S(1)}, f32[2,64]{1,0:T(2,128)}, u32[]{:S(2)}) copy-start(f32[2,64]{1,0:T(2,128)} %copy-done.20) | copy-start | bytes 1540
  1346.4 118.2 %copy-start.23 = (f32[2,64]{1,0:T(2,128)S(1)}, f32[2,64]{1,0:T(2,128)}, u32[]{:S(2)}) copy-start(f32[2,64]{1,0:T(2,128)} %copy-done.22) | copy-start | bytes 1540
  (20 other events, 39.2 us)
Sparse Core Ops, SparseCore 0:
  120.4 25.2 all-gather.4
  457.0 27.9 all-gather.6
  814.7 26.7 all-gather.8
  1192.9 28.0 all-gather.10
where the time goes:
time: 1490 us; the launch traced here: 1480 us
  blocking collectives  1170 us (79%)
  other arithmetic  103 us (7%)
  local copies, waits for them, and re-layouts  97.3 us (7%)
  between operations  48.1 us (3%)
  matrix products  38.6 us (3%)
  starting transfers between devices  22.4 us (2%)
    psum x4, blocking collectives, per_device(): lax.psum((partial_sum, edge_full), ('sec', 'ch'))  395 us
    psum x4, blocking collectives, per_device(): proj_real, proj_imag = lax.psum((loc_real, loc_imag), ('sec', 'ch'))  382 us
    psum x3, blocking collectives, per_device(): lax.psum(jnp.sum(w_outer * w_outer) + jnp.sum(w_inner * w_inner), ('sec',...  285 us
    psum x1, blocking collectives, per_device(): start_sq = lax.psum(local_sq, ('sec', 'ch'))  106 us
    gather x8, local copies, waits for them, and re-layouts, per_device(): picked = jnp.take(grouped, local_cols, axis=1)  30.6 us
  transfers between devices with their start and end apart: 12, of which 0 were waited for; matrix products, arithmetic and copies ran while one was open for 6% of the time, Pallas kernels for 0%

commit v1 on v0

v1 whole, which is shorter than its diff:
```python
import jax
import jax.numpy as jnp
import numpy as np
from jax import lax
from jax.sharding import PartitionSpec as P

ITERS = 4


inner_radius = 20.0
grid_step = 0.08
time_step = 0.01
stencil_scale = 1.0 / (24.0 * grid_step * grid_step)
taylor_terms = 10
squarings = 7
highest = lax.Precision.HIGHEST


def radial_factor(kind_map, polar_map, laser_field, radius):
    radius_ratio = inner_radius / radius
    dipole_like = radius_ratio * radius_ratio
    quadrupole_like = dipole_like * radius_ratio
    chosen = jnp.sum(
        jnp.where(polar_map[..., None] == jnp.arange(3, dtype=jnp.int32), laser_field, 0.0), axis=-1
    )
    laser_term = chosen[..., None] * radius
    kind_wide = kind_map[..., None]
    return jnp.where(
        kind_wide == 0, dipole_like, jnp.where(kind_wide == 1, quadrupole_like, laser_term)
    )


def halo(x, axis, width):
    size, length = lax.axis_size(axis), x.shape[2]
    up = [(i, i + 1) for i in range(size - 1)]
    down = [(j, i) for i, j in up]
    before = lax.ppermute(x[:, :, length - width :], axis, up)
    after = lax.ppermute(x[:, :, :width], axis, down)
    return jnp.concatenate([before, x, after], axis=2)


def kinetic(padded):
    return stencil_scale * (
        padded[:, :, :-4]
        - 16.0 * padded[:, :, 1:-3]
        + 30.0 * padded[:, :, 2:-2]
        - 16.0 * padded[:, :, 3:-1]
        + padded[:, :, 4:]
    )


def propagate(hess):
    scaled_block = jnp.zeros((2 * ITERS, 2 * ITERS), jnp.float32)
    for (i, j), (real, imag) in hess.items():
        for value, places in (
            (imag, ((i, j, 1.0), (i + ITERS, j + ITERS, 1.0))),
            (real, ((i, j + ITERS, 1.0), (i + ITERS, j, -1.0))),
        ):
            mask = np.zeros((2 * ITERS, 2 * ITERS), np.float32)
            for a, b, sign in places:
                mask[a, b] = sign
            scaled_block = scaled_block + (time_step * value) * mask
    scaled_block = scaled_block / 2.0**squarings
    identity = jnp.eye(2 * ITERS, dtype=jnp.float32)
    series = identity
    for degree in range(taylor_terms, 0, -1):
        series = identity + jnp.dot(scaled_block, series, precision=highest) / degree
    for repeat in range(squarings):
        series = jnp.dot(series, series, precision=highest)
    return (series[:ITERS, 0], series[ITERS:, 0])


def combine(scale, vector, terms):
    real, imag = (scale * vector[0], scale * vector[1])
    for (coef_real, coef_imag), other in terms:
        real = real - (coef_real * other[0] - coef_imag * other[1])
        imag = imag - (coef_real * other[1] + coef_imag * other[0])
    return jnp.stack([real, imag])


def per_device(
    outer_wave,
    inner_wave,
    surface,
    energies,
    coefficients,
    block_cols,
    block_kind,
    polarisation,
    laser_field,
):
    sec_index = lax.axis_index("sec")
    ch_index = lax.axis_index("ch")
    ch_count = lax.axis_size("ch")
    ch_dev = outer_wave.shape[1]
    rad_dev = outer_wave.shape[2]
    block_size = coefficients.shape[2]
    rows_dev = coefficients.shape[0]
    positions = sec_index * rad_dev + jnp.arange(rad_dev, dtype=jnp.int32)
    radius = inner_radius + (positions + 1).astype(jnp.float32) * grid_step
    first_sector = (sec_index == 0).astype(jnp.float32)
    local_cols = lax.dynamic_slice_in_dim(block_cols, ch_index * rows_dev, rows_dev, 0)
    local_kind = lax.dynamic_slice_in_dim(block_kind, ch_index * rows_dev, rows_dev, 0)
    local_polar = lax.dynamic_slice_in_dim(polarisation, ch_index * rows_dev, rows_dev, 0)
    local_factor = radial_factor(local_kind, local_polar, laser_field, radius)
    lane = lax.broadcasted_iota(jnp.int32, (1, 1, rad_dev), 2)

    def local_part(vector):
        outer, inner = vector
        full_rows = lax.all_gather(outer, "ch", axis=1, tiled=True)
        grouped = full_rows.reshape(2, -1, block_size, rad_dev)
        picked = jnp.take(grouped, local_cols, axis=1)
        product = jnp.einsum("lsab,xlsbr->xlsar", coefficients, picked, precision=highest)
        image = kinetic(halo(outer, "sec", 2)) + jnp.sum(
            product * local_factor[None, :, :, None, :], axis=2
        ).reshape(2, ch_dev, rad_dev)
        return (image, energies * inner)

    def with_boundary(image, ghosts, edges):
        outer, inner = image
        at_zero = (-16.0 * ghosts[:, 0] + ghosts[:, 1]) * (stencil_scale * first_sector)
        at_one = ghosts[:, 0] * (stencil_scale * first_sector)
        rim = jnp.where(
            lane == 0, at_zero[:, :, None], jnp.where(lane == 1, at_one[:, :, None], 0.0)
        )
        mixed = jnp.stack([-16.0 * edges[:, 0] + edges[:, 1], edges[:, 0]], axis=1)
        inner_add = jnp.einsum("xlc,lkc->xk", mixed, surface, precision=highest)
        return (outer + rim, inner + stencil_scale * inner_add)

    def reduce_all(vector, scalars):
        outer, inner = vector
        partial_sum = jnp.einsum("xk,lkc->xlc", inner, surface, precision=highest)
        edge_pair = jnp.stack([outer[:, :, 0], outer[:, :, 1]], axis=1) * first_sector
        edge_blank = jnp.zeros((2, 2, ch_dev * ch_count), jnp.float32)
        edge_full = lax.dynamic_update_slice_in_dim(edge_blank, edge_pair, ch_index * ch_dev, 2)
        sums, edges, totals = lax.psum(
            (partial_sum, edge_full, jnp.stack(scalars)), ("sec", "ch")
        )
        ghosts = lax.dynamic_slice_in_dim(sums, ch_index * ch_dev, ch_dev, 2)
        return (ghosts, edges, totals)

    def norm_of(vector):
        return jnp.sum(vector[0] * vector[0]) + jnp.sum(vector[1] * vector[1])

    def product_of(a, b):
        real = jnp.sum(a[0] * b[0]) + jnp.sum(a[1] * b[1])
        imag = jnp.sum(a[0][0] * b[0][1] - a[0][1] * b[0][0]) + jnp.sum(
            a[1][0] * b[1][1] - a[1][1] * b[1][0]
        )
        return [real, imag]

    current = (outer_wave, inner_wave)
    image = local_part(current)
    ghosts, edges, totals = reduce_all(current, [norm_of(current)])
    norms = [jnp.sqrt(totals[0] + 1e-06)]
    basis, images, rims = [current], [image], [(ghosts, edges)]
    hess = {}
    for column in range(ITERS):
        applied = with_boundary(images[column], *rims[column])
        scalars = []
        for vector in basis:
            scalars += product_of(vector, applied)
        scalars.append(norm_of(basis[column]))
        if column + 1 < ITERS:
            applied_image = local_part(applied)
            ghosts, edges, totals = reduce_all(applied, scalars)
        else:
            totals = lax.psum(jnp.stack(scalars), ("sec", "ch"))
        if column:
            norms.append(jnp.sqrt(totals[2 * column + 2] + 1e-06))
            hess[column, column - 1] = (norms[column], jnp.zeros((), jnp.float32))
        terms = []
        for row in range(column + 1):
            scale = 1.0 / (norms[row] * norms[column])
            real, imag = (totals[2 * row] * scale, totals[2 * row + 1] * scale)
            hess[row, column] = (real, imag)
            terms.append((real / norms[row], imag / norms[row]))
        if column + 1 < ITERS:
            inverse = 1.0 / norms[column]

            def advance(new, olds):
                return combine(inverse, new, list(zip(terms, olds)))

            basis.append(
                tuple(advance(applied[k], [old[k] for old in basis]) for k in range(2))
            )
            images.append(
                tuple(advance(applied_image[k], [old[k] for old in images]) for k in range(2))
            )
            new_rim = (ghosts, edges)
            rims.append(tuple(advance(new_rim[k], [old[k] for old in rims]) for k in range(2)))
    coef_real, coef_imag = propagate(hess)
    outputs = []
    for k in range(2):
        terms = []
        for column in range(ITERS):
            scale = norms[0] / norms[column]
            terms.append(((-coef_real[column] * scale, -coef_imag[column] * scale), basis[column][k]))
        outputs.append(combine(0.0, basis[0][k], terms))
    return tuple(outputs)


def solution(mesh):
    placed = (
        P(None, "ch", "sec"),
        P(None, ("sec", "ch")),
        P(None, ("sec", "ch"), None),
        P(("sec", "ch")),
        P("ch", None, None, None),
        P(),
        P(),
        P(),
        P(),
    )
    return jax.shard_map(
        per_device,
        mesh=mesh,
        in_specs=placed,
        out_specs=(P(None, "ch", "sec"), P(None, ("sec", "ch"))),
        check_vma=False,
    )
```

time: 1490 us -> 756 us (0.51)
  blocking collectives: 1170 us -> 494 us
  other arithmetic: 103 us -> 59 us
  local copies, waits for them, and re-layouts: 97.3 us -> 68.4 us
  between operations: 48.1 us -> 66.4 us
    psum x12 -> x5, blocking collectives: 1170 us -> 494 us  [the longest x4 396 us: reduce_all(): lax.psum((partial_sum, edge_full, jnp.stack(scalars)), ('sec', 'ch'))]
    scatter x11 -> x0, local copies, waits for them, and re-layouts: 16.8 us -> none  [the longest x4 7.57 us: per_device(): hess_imag = hess_imag.at[:column + 1, column].set(proj_imag)]
    reduce_sum x20 -> x14, other arithmetic: 37.1 us -> 25.2 us  [the longest x5 8.57 us: product_of(): jnp.sum(a[0][0] * b[0][1] - a[0][1] * b[0][0])]
    dot_general x16 -> x12, matrix products: 35.6 us -> 32.7 us  [the longest x4 21.4 us: local_part(): jnp.einsum('lsab,xlsbr->xlsar', coefficients, picked, precision=highest)]
  transfers between devices with their start and end apart: 12 -> 12, of which waited for: 0 -> 1; matrix products, arithmetic and copies ran while one was open for 6% -> 16% of each run, Pallas kernels for 0% -> 0%
where the time goes in v1:
time: 756 us; the launch traced here: 753 us
  blocking collectives  494 us (65%)
  local copies, waits for them, and re-layouts  68.4 us (9%)
  between operations  66.4 us (9%)
  other arithmetic  59 us (8%)
  matrix products  35 us (5%)
  starting transfers between devices  26.7 us (4%)
    psum x4, blocking collectives, reduce_all(): lax.psum((partial_sum, edge_full, jnp.stack(scalars)), ('sec', 'ch'))  396 us
    psum x1, blocking collectives, per_device(): totals = lax.psum(jnp.stack(scalars), ('sec', 'ch'))  98.1 us
    gather x8, local copies, waits for them, and re-layouts, local_part(): picked = jnp.take(grouped, local_cols, axis=1)  30 us
    dot_general x4, matrix products, local_part(): jnp.einsum('lsab,xlsbr->xlsar', coefficients, picked, precision=highest)  21.4 us
    ppermute x4, starting transfers between devices, halo(): after = lax.ppermute(x[:, :, :width], axis, down)  15.7 us
  transfers between devices with their start and end apart: 12, of which 1 were waited for; matrix products, arithmetic and copies ran while one was open for 16% of the time, Pallas kernels for 0%

profile of v1, /device:TPU:1, one launch (start us, length us, event | category | flops | bytes accessed | tf_op | source)
XLA Modules:
  0.0 753.0 jit_solution(13479109900754785134)
XLA Ops:
  10.1 8.7 %collective-permute-start.1 = (f32[2,384,2]{2,1,0:T(8,128)}, f32[2,384,2]{2,1,0:T(8,128)}, u32[]{:S(2)}, u32[]{:S(2)}) collective-permute-start(f32[2,384,2]{2,1,0:T(8,128)} %get-tuple-element.119), channel_id=1, source_target_pairs={{4,0},{8,4},{12,8},{16,12},{20,16},{24,20},{28,24},{32,28},{36,32}... | collective-permute-start | bytes 18440 | tf_op jit(solution)/shard_map/ppermute | solution.py:38
  25.5 103.6 %all-reduce.3 = (f32[2,2,1536]{2,1,0:T(2,128)S(1)}, f32[2,2,1536]{2,1,0:T(2,128)S(1)}) all-reduce(f32[2,2,1536]{2,1,0:T(2,128)S(1)} %copy.1182, f32[2,2,1536]{2,1,0:T(2,128)S(1)} %fusion.157), channel_id=1, replica_groups=mesh['sec'=128,'ch'=4] {'sec','ch'}, use_global_device_ids=true, to_apply=%region_2.4 | all-reduce | flops 12288 | bytes 98304 | tf_op jit(solution)/shard_map/psum | solution.py:136
  129.3 2.6 multiply_reduce_fusion.31
  139.5 3.8 gather_fusion
  143.3 3.6 copy.1177
  146.9 4.8 multiply_reduce_fusion.3
  151.9 3.9 multiply_reduce_fusion.17
  165.1 95.9 %all-reduce.2 = (f32[3]{0:T(128)S(1)}, f32[1]{0:T(128)}, f32[2,2,1536]{2,1,0:T(2,128)S(1)}, f32[2,2,1536]{2,1,0:T(2,128)S(1)}) all-reduce(f32[3]{0:T(128)S(1)} %pad_maximum_fusion.25, f32[1]{0:T(128)} %bitcast.21, f32[2,2,1536]{2,1,0:T(2,128)S(1)} %copy-done.36, ...), channel_id=1, replica_groups=mesh['sec'=128,'ch'=4] {'sec','ch'}, use_global_device_ids=true, to_apply=%region_10.12 | all-reduce | flops 12292 | bytes 98336 | tf_op jit(solution)/shard_map/psum | solution.py:136
  263.6 3.2 collective-permute-start.2
  275.5 4.1 gather_fusion.1
  279.6 3.6 copy.1188
  283.2 5.5 multiply_reduce_fusion.2
  290.6 2.3 fusion.72
  294.0 2.4 multiply_reduce_fusion.13
  298.1 2.6 fusion.118
  311.7 98.2 %all-reduce.1 = (f32[5]{0:T(128)}, f32[2,2,1536]{2,1,0:T(2,128)}, f32[2,2,1536]{2,1,0:T(2,128)}) all-reduce(f32[5]{0:T(128)} %stack.232, f32[2,2,1536]{2,1,0:T(2,128)} %copy.1198, f32[2,2,1536]{2,1,0:T(2,128)} %fusion.159), channel_id=1, replica_groups=mesh['sec'=128,'ch'=4] {'sec','ch'}, use_global_device_ids=true, to_apply=%region_25.27 | all-reduce | flops 12293 | bytes 98344 | tf_op jit(solution)/shard_map/psum | solution.py:136
  414.8 3.0 collective-permute-start.4
  425.1 2.6 multiply_reduce_fusion.23
  431.8 3.9 gather_fusion.2
  435.7 3.6 copy.1196
  439.3 5.6 multiply_reduce_fusion.1
  446.8 2.3 fusion.63
  455.3 2.7 fusion.104
  468.0 98.1 %all-reduce = (f32[7]{0:T(128)}, f32[2,2,1536]{2,1,0:T(2,128)}, f32[2,2,1536]{2,1,0:T(2,128)}) all-reduce(f32[7]{0:T(128)} %stack.248, f32[2,2,1536]{2,1,0:T(2,128)} %copy.1206, f32[2,2,1536]{2,1,0:T(2,128)} %fusion.160), channel_id=1, replica_groups=mesh['sec'=128,'ch'=4] {'sec','ch'}, use_global_device_ids=true, to_apply=%region_43.45 | all-reduce | flops 12295 | bytes 98360 | tf_op jit(solution)/shard_map/psum | solution.py:136
  574.8 2.8 collective-permute-start.6
  577.6 2.6 collective-permute-start.7
  593.4 2.7 all-gather.11.cloned.1.call-done
  596.1 3.8 gather_fusion.3
  599.9 3.6 copy.1204
  603.5 5.5 multiply_reduce_fusion
  611.1 2.4 fusion.54
  629.9 98.1 %psum.103 = f32[9]{0:T(128)S(1)} all-reduce(f32[9]{0:T(128)S(1)} %stack.266), channel_id=1, replica_groups=mesh['sec'=128,'ch'=4] {'sec','ch'}, use_global_device_ids=true, to_apply=%region_65.67 | all-reduce | flops 9 | bytes 72 | tf_op jit(solution)/shard_map/psum | solution.py:168
  (300 shorter events, 94.5 us)
Async XLA Ops:
  7.2 139.8 %copy-start = (f32[3,8,128,128]{3,2,1,0:T(8,128)S(1)}, f32[3,8,128,128]{3,2,1,0:T(8,128)}, u32[]{:S(2)}) copy-start(f32[3,8,128,128]{3,2,1,0:T(8,128)} %param.41) | copy-start | bytes 4718596
  7.2 126.1 %copy-start.1 = (f32[2,384,128]{2,1,0:T(8,128)S(1)}, f32[2,384,128]{2,1,0:T(8,128)}, u32[]{:S(2)}) copy-start(f32[2,384,128]{2,1,0:T(8,128)} %param.37) | copy-start | bytes 1179652
  7.2 17.9 %copy-start.66 = (s32[12,8]{0,1:T(8,128)S(1)}, s32[12,8]{0,1:T(8,128)}, u32[]{:S(2)}) copy-start(s32[12,8]{0,1:T(8,128)} %param.44) | copy-start | bytes 1156
  7.2 132.3 %all-gather.5.cloned.1.call-start = ((), (), s32[]{:S(2)}) async-start(), calls=%async_computation | async-start | bytes 1966080 | tf_op jit(solution)/shard_map/all_gather | solution.py:110
  8.0 267.6 %all-gather.7.cloned.1.call-start = ((), (), s32[]{:S(2)}) async-start(), calls=%async_computation.1 | async-start | bytes 1966080 | tf_op jit(solution)/shard_map/all_gather | solution.py:110
  10.1 127.6 %collective-permute-start.1 = (f32[2,384,2]{2,1,0:T(8,128)}, f32[2,384,2]{2,1,0:T(8,128)}, u32[]{:S(2)}, u32[]{:S(2)}) collective-permute-start(f32[2,384,2]{2,1,0:T(8,128)} %get-tuple-element.119), channel_id=1, source_target_pairs={{4,0},{8,4},{12,8},{16,12},{20,16},{24,20},{28,24},{32,28},{36,32}... | collective-permute-start | bytes 18440 | tf_op jit(solution)/shard_map/ppermute | solution.py:38
  18.9 133.0 %collective-permute-start = (f32[2,384,2]{2,1,0:T(8,128)}, f32[2,384,2]{2,1,0:T(8,128)}, u32[]{:S(2)}, u32[]{:S(2)}) collective-permute-start(f32[2,384,2]{2,1,0:T(8,128)} %get-tuple-element.118), channel_id=1, source_target_pairs={{0,4},{4,8},{8,12},{12,16},{16,20},{20,24},{24,28},{28,32},{32,36}... | collective-permute-start | bytes 18440 | tf_op jit(solution)/shard_map/ppermute | solution.py:37
  23.5 112.4 %copy-start.67 = (f32[128]{0:T(128)S(1)}, f32[128]{0:T(128)}, u32[]{:S(2)}) copy-start(f32[128]{0:T(128)} %get-tuple-element.196) | copy-start | bytes 1540
  23.5 112.4 %copy-start.68 = (f32[128]{0:T(128)S(1)}, f32[128]{0:T(128)}, u32[]{:S(2)}) copy-start(f32[128]{0:T(128)} %get-tuple-element.197) | copy-start | bytes 1540
  23.5 112.4 %copy-start.69 = (f32[128]{0:T(128)S(1)}, f32[128]{0:T(128)}, u32[]{:S(2)}) copy-start(f32[128]{0:T(128)} %fusion.242) | copy-start | bytes 1540
  25.5 117.9 %copy-start.39 = (s32[1024]{0:T(1024)}, s32[1024]{0:T(1024)S(1)}, u32[]{:S(2)}) copy-start(s32[1024]{0:T(1024)S(1)} %pad_clamp_fusion) | copy-start | bytes 12292
  151.9 118.9 %copy-start.46 = (f32[2,64]{1,0:T(2,128)S(1)}, f32[2,64]{1,0:T(2,128)}, u32[]{:S(2)}) copy-start(f32[2,64]{1,0:T(2,128)} %copy-done.45) | copy-start | bytes 1540
  151.9 119.0 %copy-start.51 = (f32[2,64]{1,0:T(2,128)S(1)}, f32[2,64]{1,0:T(2,128)}, u32[]{:S(2)}) copy-start(f32[2,64]{1,0:T(2,128)} %broadcast_multiply_fusion.7) | copy-start | bytes 1540
  151.9 119.0 %copy-start.65 = (f32[2,64]{1,0:T(2,128)S(1)}, f32[2,64]{1,0:T(2,128)}, u32[]{:S(2)}) copy-start(f32[2,64]{1,0:T(2,128)} %get-tuple-element.164) | copy-start | bytes 1540
  151.9 119.0 %copy-start.30 = (f32[2,2,1536]{2,1,0:T(2,128)S(1)}, f32[2,2,1536]{2,1,0:T(2,128)}, u32[]{:S(2)}) copy-start(f32[2,2,1536]{2,1,0:T(2,128)} %copy-done.29) | copy-start | bytes 73732
  151.9 119.1 %copy-start.60 = (f32[64]{0:T(128)S(1)}, f32[64]{0:T(128)}, u32[]{:S(2)}) copy-start(f32[64]{0:T(128)} %param.40) | copy-start | bytes 772
  155.8 119.6 %copy-start.6 = (f32[2,384,128]{2,1,0:T(8,128)S(1)}, f32[2,384,128]{2,1,0:T(8,128)}, u32[]{:S(2)}) copy-start(f32[2,384,128]{2,1,0:T(8,128)} %get-tuple-element.98) | copy-start | bytes 1179652
  155.8 275.9 %all-gather.9.cloned.1.call-start = ((), (), s32[]{:S(2)}) async-start(), calls=%async_computation.2 | async-start | bytes 1966080 | tf_op jit(solution)/shard_map/all_gather | solution.py:110
  263.6 27.0 %collective-permute-start.2 = (f32[2,384,2]{2,1,0:T(8,128)}, f32[2,384,2]{2,1,0:T(8,128)}, u32[]{:S(2)}, u32[]{:S(2)}) collective-permute-start(f32[2,384,2]{2,1,0:T(8,128)} %get-tuple-element.116), channel_id=1, source_target_pairs={{0,4},{4,8},{8,12},{12,16},{16,20},{20,24},{24,28},{28,32},{32,36}... | collective-permute-start | bytes 18440 | tf_op jit(solution)/shard_map/ppermute | solution.py:37
  266.8 23.8 %collective-permute-start.3 = (f32[2,384,2]{2,1,0:T(8,128)}, f32[2,384,2]{2,1,0:T(8,128)}, u32[]{:S(2)}, u32[]{:S(2)}) collective-permute-start(f32[2,384,2]{2,1,0:T(8,128)} %get-tuple-element.117), channel_id=1, source_target_pairs={{4,0},{8,4},{12,8},{16,12},{20,16},{24,20},{28,24},{32,28},{36,32}... | collective-permute-start | bytes 18440 | tf_op jit(solution)/shard_map/ppermute | solution.py:38
  275.5 18.5 %copy-start.7 = (f32[1,384,128]{2,1,0:T(8,128)}, f32[1,384,128]{2,1,0:T(8,128)S(1)}, u32[]{:S(2)}) copy-start(f32[1,384,128]{2,1,0:T(8,128)S(1)} %get-tuple-element.110) | copy-start | bytes 589828
  275.5 18.5 %copy-start.10 = (f32[1,384,128]{2,1,0:T(8,128)}, f32[1,384,128]{2,1,0:T(8,128)S(1)}, u32[]{:S(2)}) copy-start(f32[1,384,128]{2,1,0:T(8,128)S(1)} %get-tuple-element.111) | copy-start | bytes 589828
  296.4 299.7 %all-gather.11.cloned.1.call-start = ((), (), s32[]{:S(2)}) async-start(), calls=%async_computation.3 | async-start | bytes 1966080 | tf_op jit(solution)/shard_map/all_gather | solution.py:110
  300.6 130.2 %copy-start.8 = (f32[1,384,128]{2,1,0:T(8,128)S(1)}, f32[1,384,128]{2,1,0:T(8,128)}, u32[]{:S(2)}) copy-start(f32[1,384,128]{2,1,0:T(8,128)} %copy-done.7) | copy-start | bytes 589828
  300.6 130.2 %copy-start.11 = (f32[1,384,128]{2,1,0:T(8,128)S(1)}, f32[1,384,128]{2,1,0:T(8,128)}, u32[]{:S(2)}) copy-start(f32[1,384,128]{2,1,0:T(8,128)} %copy-done.10) | copy-start | bytes 589828
  414.8 32.0 %collective-permute-start.4 = (f32[2,384,2]{2,1,0:T(8,128)}, f32[2,384,2]{2,1,0:T(8,128)}, u32[]{:S(2)}, u32[]{:S(2)}) collective-permute-start(f32[2,384,2]{2,1,0:T(8,128)} %get-tuple-element.114), channel_id=1, source_target_pairs={{0,4},{4,8},{8,12},{12,16},{16,20},{20,24},{24,28},{28,32},{32,36}... | collective-permute-start | bytes 18440 | tf_op jit(solution)/shard_map/ppermute | solution.py:37
  417.8 28.9 %collective-permute-start.5 = (f32[2,384,2]{2,1,0:T(8,128)}, f32[2,384,2]{2,1,0:T(8,128)}, u32[]{:S(2)}, u32[]{:S(2)}) collective-permute-start(f32[2,384,2]{2,1,0:T(8,128)} %get-tuple-element.115), channel_id=1, source_target_pairs={{4,0},{8,4},{12,8},{16,12},{20,16},{24,20},{28,24},{32,28},{36,32}... | collective-permute-start | bytes 18440 | tf_op jit(solution)/shard_map/ppermute | solution.py:38
  452.4 116.0 %copy-start.3 = (f32[2,384,128]{2,1,0:T(8,128)}, f32[2,384,128]{2,1,0:T(8,128)S(1)}, u32[]{:S(2)}) copy-start(f32[2,384,128]{2,1,0:T(8,128)S(1)} %get-tuple-element.86) | copy-start | bytes 1179652
  568.4 23.1 %copy-start.4 = (f32[2,384,128]{2,1,0:T(8,128)S(1)}, f32[2,384,128]{2,1,0:T(8,128)}, u32[]{:S(2)}) copy-start(f32[2,384,128]{2,1,0:T(8,128)} %copy-done.3) | copy-start | bytes 1179652
  574.8 36.2 %collective-permute-start.6 = (f32[2,384,2]{2,1,0:T(8,128)}, f32[2,384,2]{2,1,0:T(8,128)}, u32[]{:S(2)}, u32[]{:S(2)}) collective-permute-start(f32[2,384,2]{2,1,0:T(8,128)} %get-tuple-element.112), channel_id=1, source_target_pairs={{0,4},{4,8},{8,12},{12,16},{16,20},{20,24},{24,28},{28,32},{32,36}... | collective-permute-start | bytes 18440 | tf_op jit(solution)/shard_map/ppermute | solution.py:37
  577.6 33.5 %collective-permute-start.7 = (f32[2,384,2]{2,1,0:T(8,128)}, f32[2,384,2]{2,1,0:T(8,128)}, u32[]{:S(2)}, u32[]{:S(2)}) collective-permute-start(f32[2,384,2]{2,1,0:T(8,128)} %get-tuple-element.113), channel_id=1, source_target_pairs={{4,0},{8,4},{12,8},{16,12},{20,16},{24,20},{28,24},{32,28},{36,32}... | collective-permute-start | bytes 18440 | tf_op jit(solution)/shard_map/ppermute | solution.py:38
  614.9 128.7 %copy-start.48 = (f32[1,64]{1,0:T(1,128)S(1)}, f32[1,64]{1,0:T(1,128)}, u32[]{:S(2)}) copy-start(f32[1,64]{1,0:T(1,128)} %copy-done.47) | copy-start | bytes 772
  (50 other events, 296.7 us)
Sparse Core Ops, SparseCore 0:
  10.1 37.0 all-gather.4
  156.0 25.3 all-gather.6
  296.6 28.8 all-gather.8
  568.5 27.5 all-gather.10

commit v2 on v1

--- a/solution.py
+++ b/solution.py
@@ -1,7 +1,11 @@
+import functools
+
 import jax
 import jax.numpy as jnp
 import numpy as np
 from jax import lax
+from jax.experimental import pallas as pl
+from jax.experimental.pallas import tpu as pltpu
 from jax.sharding import PartitionSpec as P
 
 ITERS = 4
@@ -30,13 +34,172 @@
     )
 
 
-def halo(x, axis, width):
-    size, length = lax.axis_size(axis), x.shape[2]
-    up = [(i, i + 1) for i in range(size - 1)]
-    down = [(j, i) for i, j in up]
-    before = lax.ppermute(x[:, :, length - width :], axis, up)
-    after = lax.ppermute(x[:, :, :width], axis, down)
-    return jnp.concatenate([before, x, after], axis=2)
+MESH = pl.DeviceIdType.MESH
+
+
+def exchange_kernel(dims, bulk, *refs):
+    y_size, z_size, c_size, x_size = dims
+    if bulk:
+        (ghost_in, edge_in, first_in, last_in, outer_in) = refs[:5]
+        (sum_out, edge_out, before_out, after_out, full_out) = refs[5:10]
+        refs = refs[10:]
+    else:
+        (ghost_in, sum_out) = refs[:2]
+        refs = refs[2:]
+    (x_slots, c_slots, z_slots, y_slots) = refs[:4]
+    (x_send, x_recv, c_send, c_recv, z_send, z_recv, y_send, y_recv) = refs[4:12]
+    if bulk:
+        (bulk_send, bulk_recv, side_send, side_recv, edge_send, edge_recv, own_sem) = refs[12:]
+    sec = lax.axis_index("sec")
+    x = lax.axis_index("ch")
+    c = lax.rem(sec, c_size)
+    z = lax.rem(sec // c_size, z_size)
+    y = sec // (c_size * z_size)
+    sec_size = y_size * z_size * c_size
+    rows = ghost_in.shape[1]
+
+    def x_peer(d):
+        return {"ch": lax.rem(x + d, x_size)}
+
+    def c_peer(d):
+        return {"sec": (y * z_size + z) * c_size + lax.rem(c + d, c_size)}
+
+    def z_peer(d):
+        return {"sec": (y * z_size + lax.rem(z + d, z_size)) * c_size + c}
+
+    def y_peer(d):
+        return {"sec": (lax.rem(y + d, y_size) * z_size + z) * c_size + c}
+
+    up = {"sec": lax.rem(sec + 1, sec_size)}
+    down = {"sec": lax.rem(sec + sec_size - 1, sec_size)}
+
+    greeted = []
+    for size, peer in ((x_size, x_peer), (c_size, c_peer), (z_size, z_peer), (y_size, y_peer)):
+        greeted += [peer(d) for d in range(1, size)]
+    if bulk:
+        greeted += [up, down]
+    barrier = pltpu.get_barrier_semaphore()
+    for peer in greeted:
+        pl.semaphore_signal(barrier, inc=1, device_id=peer, device_id_type=MESH)
+    pl.semaphore_wait(barrier, len(greeted))
+
+    def remote(src, dst, send, recv, peer):
+        copy = pltpu.make_async_remote_copy(
+            src_ref=src,
+            dst_ref=dst,
+            send_sem=send,
+            recv_sem=recv,
+            device_id=peer,
+            device_id_type=MESH,
+        )
+        copy.start()
+        return copy
+
+    x_copies = []
+    for d in range(1, x_size):
+        x_copies.append(
+            remote(
+                ghost_in.at[lax.rem(x + d, x_size)],
+                x_slots.at[x],
+                x_send.at[d - 1],
+                x_recv.at[d - 1],
+                x_peer(d),
+            )
+        )
+    later = []
+    if bulk:
+        later.append(remote(last_in, before_out, side_send.at[0], side_recv.at[0], up))
+        later.append(remote(first_in, after_out, side_send.at[1], side_recv.at[1], down))
+        for d in range(1, x_size):
+            later.append(
+                remote(
+                    outer_in, full_out.at[x], bulk_send.at[d - 1], bulk_recv.at[d - 1], x_peer(d)
+                )
+            )
+        own = pltpu.make_async_copy(outer_in, full_out.at[x], own_sem)
+        own.start()
+        later.append(own)
+    x_slots[x] = ghost_in[x]
+    for copy in x_copies:
+        copy.wait()
+
+    def total(slots, size):
+        value = slots[0]
+        for k in range(1, size):
+            value = value + slots[k]
+        return value
+
+    c_slots[c, 0:rows] = total(x_slots, x_size)
+    if bulk:
+        c_slots[c, rows:] = edge_in[...]
+
+    def stage(slots, me, size, peer, send, recv):
+        copies = []
+        for d in range(1, size):
+            copies.append(
+                remote(slots.at[me], slots.at[me], send.at[d - 1], recv.at[d - 1], peer(d))
+            )
+        for copy in copies:
+            copy.wait()
+        return total(slots, size)
+
+    z_slots[z] = stage(c_slots, c, c_size, c_peer, c_send, c_recv)
+    y_slots[y] = stage(z_slots, z, z_size, z_peer, z_send, z_recv)
+    value = stage(y_slots, y, y_size, y_peer, y_send, y_recv)
+    sum_out[...] = value[0:rows]
+    if bulk:
+        edge_out[x] = value[rows:]
+        copies = []
+        for d in range(1, x_size):
+            copies.append(
+                remote(
+                    edge_out.at[x],
+                    edge_out.at[x],
+                    edge_send.at[d - 1],
+                    edge_recv.at[d - 1],
+                    x_peer(d),
+                )
+            )
+        for copy in copies + later:
+            copy.wait()
+
+
+def exchange(dims, ghosts, edges=None, first=None, last=None, outer=None):
+    bulk = outer is not None
+    y_size, z_size, c_size, x_size = dims
+    x_count, rows, lanes = ghosts.shape
+    vmem = pl.BlockSpec(memory_space=pltpu.VMEM)
+    hbm = pl.BlockSpec(memory_space=pl.ANY)
+    shape = functools.partial(jax.ShapeDtypeStruct, dtype=jnp.float32)
+    outs = [shape((rows, lanes))]
+    args = [ghosts]
+    width = rows
+    if bulk:
+        args += [edges, first, last, outer]
+        side = edges.shape
+        width = rows + side[0]
+        outs += [shape((x_size,) + side), shape(side), shape(side), shape((x_size,) + outer.shape)]
+    dma = pltpu.SemaphoreType.DMA
+    scratch = [
+        pltpu.VMEM((x_size, rows, lanes), jnp.float32),
+        pltpu.VMEM((c_size, width, lanes), jnp.float32),
+        pltpu.VMEM((z_size, width, lanes), jnp.float32),
+        pltpu.VMEM((y_size, width, lanes), jnp.float32),
+    ]
+    for size in (x_size, c_size, z_size, y_size):
+        scratch += [dma((size - 1,)), dma((size - 1,))]
+    if bulk:
+        scratch += [dma((x_size - 1,)), dma((x_size - 1,)), dma((2,)), dma((2,))]
+        scratch += [dma((x_size - 1,)), dma((x_size - 1,)), dma]
+    return pl.pallas_call(
+        functools.partial(exchange_kernel, dims, bulk),
+        out_shape=outs,
+        in_specs=[vmem] * len(args),
+        out_specs=[vmem] * 4 + [hbm] if bulk else [vmem],
+        scratch_shapes=scratch,
+        compiler_params=pltpu.CompilerParams(collective_id=1 if bulk else 2, has_side_effects=True),
+        name="exchange_bulk" if bulk else "exchange_sums",
+    )(*args)
 
 
 def kinetic(padded):
@@ -79,6 +242,7 @@
 
 
 def per_device(
+    dims,
     outer_wave,
     inner_wave,
     surface,
@@ -99,22 +263,59 @@
     positions = sec_index * rad_dev + jnp.arange(rad_dev, dtype=jnp.int32)
     radius = inner_radius + (positions + 1).astype(jnp.float32) * grid_step
     first_sector = (sec_index == 0).astype(jnp.float32)
+    last_sector = (sec_index == lax.axis_size("sec") - 1).astype(jnp.float32)
+    pair_rows = 4 * ch_dev // 128
+    side_rows = (pair_rows // 8 + 1) * 8
     local_cols = lax.dynamic_slice_in_dim(block_cols, ch_index * rows_dev, rows_dev, 0)
     local_kind = lax.dynamic_slice_in_dim(block_kind, ch_index * rows_dev, rows_dev, 0)
     local_polar = lax.dynamic_slice_in_dim(polarisation, ch_index * rows_dev, rows_dev, 0)
     local_factor = radial_factor(local_kind, local_polar, laser_field, radius)
     lane = lax.broadcasted_iota(jnp.int32, (1, 1, rad_dev), 2)
 
-    def local_part(vector):
+    def padded_rows(value, count):
+        return jnp.concatenate([value, jnp.zeros((count - value.shape[0], 128), jnp.float32)], axis=0)
+
+    def column_rows(outer, start):
+        pair = jnp.stack([outer[:, :, start], outer[:, :, start + 1]], axis=1)
+        return padded_rows(pair.reshape(pair_rows, 128), side_rows)
+
+    def side_columns(rows, keep):
+        pair = rows[:pair_rows].reshape(2, 2, ch_dev) * keep
+        return jnp.transpose(pair, (0, 2, 1))
+
+    def scalar_row(scalars):
+        place = lax.broadcasted_iota(jnp.int32, (1, 128), 1)
+        row = jnp.zeros((1, 128), jnp.float32)
+        for k, value in enumerate(scalars):
+            row = jnp.where(place == k, value, row)
+        return row
+
+    def exchanged(vector, scalars):
         outer, inner = vector
-        full_rows = lax.all_gather(outer, "ch", axis=1, tiled=True)
-        grouped = full_rows.reshape(2, -1, block_size, rad_dev)
-        picked = jnp.take(grouped, local_cols, axis=1)
-        product = jnp.einsum("lsab,xlsbr->xlsar", coefficients, picked, precision=highest)
-        image = kinetic(halo(outer, "sec", 2)) + jnp.sum(
+        partial_sum = jnp.einsum("xk,lkc->xlc", inner, surface, precision=highest)
+        sliced = jnp.transpose(partial_sum.reshape(2, 2, ch_count, ch_dev), (2, 0, 1, 3))
+        sliced = sliced.reshape(ch_count, pair_rows, 128)
+        tail = padded_rows(scalar_row(scalars), side_rows - pair_rows)
+        tail = jnp.broadcast_to(tail[None], (ch_count,) + tail.shape)
+        first = column_rows(outer, 0)
+        last = column_rows(outer, rad_dev - 2)
+        sums, edge_rows, before, after, full = exchange(
+            dims, jnp.concatenate([sliced, tail], axis=1), first * first_sector, first, last, outer
+        )
+        ghosts = sums[:pair_rows].reshape(2, 2, ch_dev)
+        edges = edge_rows[:, :pair_rows].reshape(ch_count, 2, 2, ch_dev)
+        edges = jnp.transpose(edges, (1, 2, 0, 3)).reshape(2, 2, ch_count * ch_dev)
+        grouped = full.reshape(ch_count, 2, rows_dev, block_size, rad_dev)
+        picked = grouped[local_cols // rows_dev, :, local_cols % rows_dev]
+        product = jnp.einsum("lsab,lsxbr->xlsar", coefficients, picked, precision=highest)
+        padded = jnp.concatenate(
+            [side_columns(before, 1.0 - first_sector), outer, side_columns(after, 1.0 - last_sector)],
+            axis=2,
+        )
+        image = kinetic(padded) + jnp.sum(
             product * local_factor[None, :, :, None, :], axis=2
         ).reshape(2, ch_dev, rad_dev)
-        return (image, energies * inner)
+        return (ghosts, edges, sums[pair_rows], (image, energies * inner))
 
     def with_boundary(image, ghosts, edges):
         outer, inner = image
@@ -127,18 +328,6 @@
         inner_add = jnp.einsum("xlc,lkc->xk", mixed, surface, precision=highest)
         return (outer + rim, inner + stencil_scale * inner_add)
 
-    def reduce_all(vector, scalars):
-        outer, inner = vector
-        partial_sum = jnp.einsum("xk,lkc->xlc", inner, surface, precision=highest)
-        edge_pair = jnp.stack([outer[:, :, 0], outer[:, :, 1]], axis=1) * first_sector
-        edge_blank = jnp.zeros((2, 2, ch_dev * ch_count), jnp.float32)
-        edge_full = lax.dynamic_update_slice_in_dim(edge_blank, edge_pair, ch_index * ch_dev, 2)
-        sums, edges, totals = lax.psum(
-            (partial_sum, edge_full, jnp.stack(scalars)), ("sec", "ch")
-        )
-        ghosts = lax.dynamic_slice_in_dim(sums, ch_index * ch_dev, ch_dev, 2)
-        return (ghosts, edges, totals)
-
     def norm_of(vector):
         return jnp.sum(vector[0] * vector[0]) + jnp.sum(vector[1] * vector[1])
 
@@ -150,8 +339,7 @@
         return [real, imag]
 
     current = (outer_wave, inner_wave)
-    image = local_part(current)
-    ghosts, edges, totals = reduce_all(current, [norm_of(current)])
+    ghosts, edges, totals, image = exchanged(current, [norm_of(current)])
     norms = [jnp.sqrt(totals[0] + 1e-06)]
     basis, images, rims = [current], [image], [(ghosts, edges)]
     hess = {}
@@ -162,10 +350,10 @@
             scalars += product_of(vector, applied)
         scalars.append(norm_of(basis[column]))
         if column + 1 < ITERS:
-            applied_image = local_part(applied)
-            ghosts, edges, totals = reduce_all(applied, scalars)
+            ghosts, edges, totals, applied_image = exchanged(applied, scalars)
         else:
-            totals = lax.psum(jnp.stack(scalars), ("sec", "ch"))
+            row = padded_rows(scalar_row(scalars), 8)
+            totals = exchange(dims, jnp.broadcast_to(row[None], (ch_count, 8, 128)))[0][0]
         if column:
             norms.append(jnp.sqrt(totals[2 * column + 2] + 1e-06))
             hess[column, column - 1] = (norms[column], jnp.zeros((), jnp.float32))
@@ -213,7 +401,7 @@
         P(),
     )
     return jax.shard_map(
-        per_device,
+        functools.partial(per_device, (8, 8, 2, 4)),
         mesh=mesh,
         in_specs=placed,
         out_specs=(P(None, "ch", "sec"), P(None, ("sec", "ch"))),

time: 756 us -> 452 us (0.60)
  blocking collectives: 494 us -> 0 us
  Pallas kernels: 0 us -> 154 us
  local copies, waits for them, and re-layouts: 68.4 us -> 105 us
  starting transfers between devices: 26.7 us -> 0 us
  other arithmetic: 59 us -> 82.3 us
  matrix products: 35 us -> 51.2 us
  between operations: 66.4 us -> 53.8 us
    psum x5 -> x0, blocking collectives: 494 us -> none  [the longest x4 396 us: reduce_all(): lax.psum((partial_sum, edge_full, jnp.stack(scalars)), ('sec', 'ch'))]
    pallas_call x0 -> x5, Pallas kernels: none -> 154 us  [exchange(): pl.pallas_call(functools.partial(exchange_kernel, dims, bulk), out_shape=...]
    ppermute x8 -> x0, starting transfers between devices: 26.6 us -> none  [the longest x4 15.7 us: halo(): after = lax.ppermute(x[:, :, :width], axis, down)]
    reshape x0 -> x30, local copies, waits for them, and re-layouts: none -> 25.8 us  [the longest x8 7.78 us: column_rows(): return padded_rows(pair.reshape(pair_rows, 128), side_rows)]
    mul x0 -> x16, local copies, waits for them, and re-layouts: none -> 19.4 us  [side_columns(): pair = rows[:pair_rows].reshape(2, 2, ch_dev) * keep]
    dot_general x8, matrix products: 23.3 us -> 38.1 us  [the longest x4 32.9 us: exchanged(): jnp.einsum('lsab,lsxbr->xlsar', coefficients, picked, precision=highest)]
    gather x8 -> x4, local copies, waits for them, and re-layouts: 30 us -> 15.6 us  [exchanged(): picked = grouped[local_cols // rows_dev, :, local_cols % rows_dev]]
    concatenate x0 -> x9, other arithmetic: none -> 9.32 us  [the longest x4 4.53 us: padded_rows(): jnp.concatenate([value, jnp.zeros((count - value.shape[0], 128), jnp.floa...]
  transfers between devices with their start and end apart: 12 -> 0, of which waited for: 1 -> 0; matrix products, arithmetic and copies ran while one was open for 16% -> 0% of each run, Pallas kernels for 0% -> 0%
where the time goes in v2:
time: 452 us; the launch traced here: 447 us
  Pallas kernels  154 us (34%)
  local copies, waits for them, and re-layouts  105 us (23%)
  other arithmetic  82.3 us (18%)
  between operations  53.8 us (12%)
  matrix products  51.2 us (11%)
    pallas_call x5, Pallas kernels, exchange(): pl.pallas_call(functools.partial(exchange_kernel, dims, bulk), out_shape=...  154 us
    dot_general x4, matrix products, exchanged(): jnp.einsum('lsab,lsxbr->xlsar', coefficients, picked, precision=highest)  32.9 us
    sub x22, other arithmetic, combine(): real = real - (coef_real * other[0] - coef_imag * other[1])  21.2 us
    mul x16, local copies, waits for them, and re-layouts, side_columns(): pair = rows[:pair_rows].reshape(2, 2, ch_dev) * keep  19.4 us
    gather x4, local copies, waits for them, and re-layouts, exchanged(): picked = grouped[local_cols // rows_dev, :, local_cols % rows_dev]  15.6 us
    dot_general x4, matrix products, with_boundary(): inner_add = jnp.einsum('xlc,lkc->xk', mixed, surface, precision=highest)  10.8 us

profile of v2, /device:TPU:1, one launch (start us, length us, event | category | flops | bytes accessed | tf_op | source)
XLA Modules:
  0.0 447.0 jit_solution(4540360138580529710)
XLA Ops:
  0.7 2.1 fusion.213
  9.6 41.7 %exchange_bulk.4 = (f32[16,128]{1,0:T(8,128)}, f32[4,16,128]{2,1,0:T(8,128)}, f32[16,128]{1,0:T(8,128)}, f32[16,128]{1,0:T(8,128)}, f32[4,2,384,128]{3,2,1,0:T(8,128)}) custom-call(f32[4,16,128]{2,1,0:T(8,128)} %pad_maximum_fusion.12.refs_0_, f32[16,128]{1,0:T(8,128)} %get-tuple-element.179.refs_1_, f32[16,128]{1,0:T(8,128)} %get-tuple-element.178.refs_2_, ...), custom_call_target="tpu_custom_call" | custom-call | tf_op jit(solution)/shard_map/exchange_bulk/pallas_call | solution.py:194
  53.6 3.9 gather_fusion
  58.1 7.6 %multiply_reduce_fusion.3 = f32[3,2,128,128]{3,2,1,0:T(8,128)S(1)} fusion(f32[3,8,2,128,128]{4,3,2,1,0:T(8,128)} %bitcast.614, f32[3,8,128,128]{3,2,1,0:T(8,128)S(1)} %copy-done, f32[3,8,128]{2,1,0:T(8,128)S(1)} %select_select_fusion), kind=kOutput, calls=%fused_computation.7 | convolution fusion | flops 1209434112 | bytes 5124096 | tf_op jit(solution)/shard_map/lsab,lsxbr->xlsar/dot_general | solution.py:310
  68.5 3.1 multiply_reduce_fusion.16
  85.8 2.7 broadcast_multiply_fusion.8
  100.9 29.5 %exchange_bulk.5 = (f32[16,128]{1,0:T(8,128)}, f32[4,16,128]{2,1,0:T(8,128)}, f32[16,128]{1,0:T(8,128)}, f32[16,128]{1,0:T(8,128)}, f32[4,2,384,128]{3,2,1,0:T(8,128)}) custom-call(f32[4,16,128]{2,1,0:T(8,128)} %pad_maximum_fusion.13.refs_0_, f32[16,128]{1,0:T(8,128)} %get-tuple-element.177.refs_1_, f32[16,128]{1,0:T(8,128)} %get-tuple-element.176.refs_2_, ...), custom_call_target="tpu_custom_call" | custom-call | tf_op jit(solution)/shard_map/exchange_bulk/pallas_call | solution.py:194
  130.4 3.9 gather_fusion.1
  134.3 8.4 %multiply_reduce_fusion.2 = f32[3,2,128,128]{3,2,1,0:T(8,128)} fusion(f32[3,8,2,128,128]{4,3,2,1,0:T(8,128)} %bitcast.616, f32[3,8,128,128]{3,2,1,0:T(8,128)S(1)} %copy-done, f32[3,8,128]{2,1,0:T(8,128)S(1)} %select_select_fusion), kind=kOutput, calls=%fused_computation.6 | convolution fusion | flops 1209434112 | bytes 5124096 | tf_op jit(solution)/shard_map/lsab,lsxbr->xlsar/dot_general | solution.py:310
  153.0 3.0 fusion.44
  164.5 2.0 multiply_reduce_fusion.15
  183.9 2.7 multiply_reduce_fusion.29
  187.9 2.0 fusion.176
  198.7 34.0 %exchange_bulk.6 = (f32[16,128]{1,0:T(8,128)}, f32[4,16,128]{2,1,0:T(8,128)}, f32[16,128]{1,0:T(8,128)}, f32[16,128]{1,0:T(8,128)}, f32[4,2,384,128]{3,2,1,0:T(8,128)}) custom-call(f32[4,16,128]{2,1,0:T(8,128)} %pad_maximum_fusion.14.refs_0_, f32[16,128]{1,0:T(8,128)} %get-tuple-element.173.refs_1_, f32[16,128]{1,0:T(8,128)} %get-tuple-element.172.refs_2_, ...), custom_call_target="tpu_custom_call" | custom-call | tf_op jit(solution)/shard_map/exchange_bulk/pallas_call | solution.py:194
  232.7 3.9 gather_fusion.2
  236.6 8.4 %multiply_reduce_fusion.1 = f32[3,2,128,128]{3,2,1,0:T(8,128)} fusion(f32[3,8,2,128,128]{4,3,2,1,0:T(8,128)} %bitcast.617, f32[3,8,128,128]{3,2,1,0:T(8,128)S(1)} %copy-done, f32[3,8,128]{2,1,0:T(8,128)S(1)} %select_select_fusion), kind=kOutput, calls=%fused_computation.5 | convolution fusion | flops 1209434112 | bytes 5124096 | tf_op jit(solution)/shard_map/lsab,lsxbr->xlsar/dot_general | solution.py:310
  255.4 3.0 fusion.35
  263.6 2.2 fusion.70
  271.8 2.2 multiply_reduce_fusion.12
  292.2 2.7 multiply_reduce_fusion.26
  296.2 2.0 fusion.164
  298.2 2.6 fusion.74
  316.2 28.6 %exchange_bulk.7 = (f32[16,128]{1,0:T(8,128)}, f32[4,16,128]{2,1,0:T(8,128)}, f32[16,128]{1,0:T(8,128)}, f32[16,128]{1,0:T(8,128)}, f32[4,2,384,128]{3,2,1,0:T(8,128)}) custom-call(f32[4,16,128]{2,1,0:T(8,128)} %pad_maximum_fusion.15.refs_0_, f32[16,128]{1,0:T(8,128)} %get-tuple-element.166.refs_1_, f32[16,128]{1,0:T(8,128)} %get-tuple-element.165.refs_2_, ...), custom_call_target="tpu_custom_call" | custom-call | tf_op jit(solution)/shard_map/exchange_bulk/pallas_call | solution.py:194
  355.3 2.7 multiply_reduce_fusion.22
  358.0 3.9 gather_fusion.3
  361.9 8.5 %multiply_reduce_fusion = f32[3,2,128,128]{3,2,1,0:T(8,128)} fusion(f32[3,8,2,128,128]{4,3,2,1,0:T(8,128)} %bitcast.615, f32[3,8,128,128]{3,2,1,0:T(8,128)S(1)} %copy-done, f32[3,8,128]{2,1,0:T(8,128)S(1)} %select_select_fusion), kind=kOutput, calls=%fused_computation.4 | convolution fusion | flops 1209434112 | bytes 5124096 | tf_op jit(solution)/shard_map/lsab,lsxbr->xlsar/dot_general | solution.py:310
  370.4 2.0 copy.348
  380.8 2.3 fusion.26
  383.1 2.1 fusion.66
  386.6 2.0 multiply_reduce_fusion.8
  391.4 2.0 fusion.84
  407.2 20.6 %exchange_sums.1 = f32[8,128]{1,0:T(8,128)} custom-call(f32[4,8,128]{2,1,0:T(8,128)} %broadcast_in_dim.312.refs_0_), custom_call_target="tpu_custom_call" | custom-call | tf_op jit(solution)/shard_map/exchange_sums/pallas_call | solution.py:194
  (308 shorter events, 144.9 us)
Async XLA Ops:
  0.6 57.4 %copy-start = (f32[3,8,128,128]{3,2,1,0:T(8,128)S(1)}, f32[3,8,128,128]{3,2,1,0:T(8,128)}, u32[]{:S(2)}) copy-start(f32[3,8,128,128]{3,2,1,0:T(8,128)} %param.39) | copy-start | bytes 4718596
  0.6 5.7 %copy-start.1 = (f32[2,384,128]{2,1,0:T(8,128)S(1)}, f32[2,384,128]{2,1,0:T(8,128)}, u32[]{:S(2)}) copy-start(f32[2,384,128]{2,1,0:T(8,128)} %refs_4_.1) | copy-start | bytes 1179652
  0.7 3.8 copy-start.22
  0.7 7.7 %copy-start.7 = (f32[2,64,1536]{2,1,0:T(8,128)S(1)}, f32[2,64,1536]{2,1,0:T(8,128)}, u32[]{:S(2)}) copy-start(f32[2,64,1536]{2,1,0:T(8,128)} %param.37) | copy-start | bytes 2359300
  53.6 4.0 copy-start.48
  53.6 4.1 copy-start.47
  57.5 9.1 %copy-start.41 = (f32[16,128]{1,0:T(8,128)S(1)}, f32[16,128]{1,0:T(8,128)}, u32[]{:S(2)}) copy-start(f32[16,128]{1,0:T(8,128)} %get-tuple-element.23) | copy-start | bytes 24580
  57.5 9.1 %copy-start.42 = (f32[16,128]{1,0:T(8,128)S(1)}, f32[16,128]{1,0:T(8,128)}, u32[]{:S(2)}) copy-start(f32[16,128]{1,0:T(8,128)} %get-tuple-element.24) | copy-start | bytes 24580
  58.1 10.4 %copy-start.2 = (f32[2,384,128]{2,1,0:T(8,128)S(1)}, f32[2,384,128]{2,1,0:T(8,128)}, u32[]{:S(2)}) copy-start(f32[2,384,128]{2,1,0:T(8,128)} %refs_4_.1) | copy-start | bytes 1179652
  68.5 4.6 %copy-start.43 = (pred[128]{0:T(512)(128)(4,1)}, pred[128]{0:T(512)(128)(4,1)S(1)}, u32[]{:S(2)}) copy-start(pred[128]{0:T(512)(128)(4,1)S(1)} %get-tuple-element.237) | copy-start | bytes 388
  68.5 4.6 %copy-start.44 = (pred[128]{0:T(512)(128)(4,1)}, pred[128]{0:T(512)(128)(4,1)S(1)}, u32[]{:S(2)}) copy-start(pred[128]{0:T(512)(128)(4,1)S(1)} %get-tuple-element.238) | copy-start | bytes 388
  71.7 29.2 %copy-start.8 = (f32[2,384,128]{2,1,0:T(8,128)}, f32[2,384,128]{2,1,0:T(8,128)S(1)}, u32[]{:S(2)}) copy-start(f32[2,384,128]{2,1,0:T(8,128)S(1)} %get-tuple-element.120.refs_4_) | copy-start | bytes 1179652
  71.7 89.3 %copy-start.16 = (f32[2,384,128]{2,1,0:T(8,128)}, f32[2,384,128]{2,1,0:T(8,128)S(1)}, u32[]{:S(2)}) copy-start(f32[2,384,128]{2,1,0:T(8,128)S(1)} %get-tuple-element.121) | copy-start | bytes 1179652
  134.3 18.7 %copy-start.9 = (f32[2,384,128]{2,1,0:T(8,128)S(1)}, f32[2,384,128]{2,1,0:T(8,128)}, u32[]{:S(2)}) copy-start(f32[2,384,128]{2,1,0:T(8,128)} %copy-done.8) | copy-start | bytes 1179652
  166.5 32.2 %copy-start.3 = (f32[2,384,128]{2,1,0:T(8,128)}, f32[2,384,128]{2,1,0:T(8,128)S(1)}, u32[]{:S(2)}) copy-start(f32[2,384,128]{2,1,0:T(8,128)S(1)} %get-tuple-element.118.refs_4_) | copy-start | bytes 1179652
  236.6 18.8 %copy-start.4 = (f32[2,384,128]{2,1,0:T(8,128)S(1)}, f32[2,384,128]{2,1,0:T(8,128)}, u32[]{:S(2)}) copy-start(f32[2,384,128]{2,1,0:T(8,128)} %copy-done.3) | copy-start | bytes 1179652
  245.0 26.0 %copy-start.11 = (f32[1,384,128]{2,1,0:T(8,128)S(1)}, f32[1,384,128]{2,1,0:T(8,128)}, u32[]{:S(2)}) copy-start(f32[1,384,128]{2,1,0:T(8,128)} %copy-done.10) | copy-start | bytes 589828
  245.0 26.0 %copy-start.14 = (f32[1,384,128]{2,1,0:T(8,128)S(1)}, f32[1,384,128]{2,1,0:T(8,128)}, u32[]{:S(2)}) copy-start(f32[1,384,128]{2,1,0:T(8,128)} %copy-done.13) | copy-start | bytes 589828
  274.0 42.2 %copy-start.5 = (f32[2,384,128]{2,1,0:T(8,128)}, f32[2,384,128]{2,1,0:T(8,128)S(1)}, u32[]{:S(2)}) copy-start(f32[2,384,128]{2,1,0:T(8,128)S(1)} %get-tuple-element.109.refs_4_) | copy-start | bytes 1179652
  355.3 6.6 %copy-start.45 = (f32[1,64]{1,0:T(1,128)}, f32[1,64]{1,0:T(1,128)S(1)}, u32[]{:S(2)}) copy-start(f32[1,64]{1,0:T(1,128)S(1)} %get-tuple-element.207) | copy-start | bytes 772
  355.3 6.6 %copy-start.46 = (f32[1,64]{1,0:T(1,128)}, f32[1,64]{1,0:T(1,128)S(1)}, u32[]{:S(2)}) copy-start(f32[1,64]{1,0:T(1,128)S(1)} %get-tuple-element.208) | copy-start | bytes 772
  361.9 18.9 %copy-start.6 = (f32[2,384,128]{2,1,0:T(8,128)S(1)}, f32[2,384,128]{2,1,0:T(8,128)}, u32[]{:S(2)}) copy-start(f32[2,384,128]{2,1,0:T(8,128)} %copy-done.5) | copy-start | bytes 1179652
  361.9 21.2 %copy-start.17 = (f32[2,384,128]{2,1,0:T(8,128)S(1)}, f32[2,384,128]{2,1,0:T(8,128)}, u32[]{:S(2)}) copy-start(f32[2,384,128]{2,1,0:T(8,128)} %copy-done.16) | copy-start | bytes 1179652
  370.4 14.8 %copy-start.24 = (f32[16,128]{1,0:T(8,128)S(1)}, f32[16,128]{1,0:T(8,128)}, u32[]{:S(2)}) copy-start(f32[16,128]{1,0:T(8,128)} %get-tuple-element.26) | copy-start | bytes 24580
  370.4 14.9 %copy-start.28 = (f32[1,2,384]{2,1,0:T(2,128)S(1)}, f32[1,2,384]{2,1,0:T(2,128)}, u32[]{:S(2)}) copy-start(f32[1,2,384]{2,1,0:T(2,128)} %copy-done.27) | copy-start | bytes 9220
  370.4 15.7 %copy-start.12 = (f32[1,384,128]{2,1,0:T(8,128)S(1)}, f32[1,384,128]{2,1,0:T(8,128)}, u32[]{:S(2)}) copy-start(f32[1,384,128]{2,1,0:T(8,128)} %copy-done.10) | copy-start | bytes 589828
  370.4 15.7 %copy-start.15 = (f32[1,384,128]{2,1,0:T(8,128)S(1)}, f32[1,384,128]{2,1,0:T(8,128)}, u32[]{:S(2)}) copy-start(f32[1,384,128]{2,1,0:T(8,128)} %copy-done.13) | copy-start | bytes 589828
  380.8 4.4 copy-start.37
  385.2 4.7 %copy-start.23 = (f32[2,64]{1,0:T(2,128)S(1)}, f32[2,64]{1,0:T(2,128)}, u32[]{:S(2)}) copy-start(f32[2,64]{1,0:T(2,128)} %param.36) | copy-start | bytes 1540
  386.6 57.5 %copy-start.34 = (f32[1,64]{1,0:T(1,128)S(1)}, f32[1,64]{1,0:T(1,128)}, u32[]{:S(2)}) copy-start(f32[1,64]{1,0:T(1,128)} %copy-done.33) | copy-start | bytes 772
  386.6 57.5 %copy-start.36 = (f32[1,64]{1,0:T(1,128)S(1)}, f32[1,64]{1,0:T(1,128)}, u32[]{:S(2)}) copy-start(f32[1,64]{1,0:T(1,128)} %copy-done.35) | copy-start | bytes 772
  386.6 57.5 %copy-start.39 = (f32[1,64]{1,0:T(1,128)S(1)}, f32[1,64]{1,0:T(1,128)}, u32[]{:S(2)}) copy-start(f32[1,64]{1,0:T(1,128)} %copy-done.38) | copy-start | bytes 772
  (17 other events, 24.4 us)

commit v3 on v2

--- a/solution.py
+++ b/solution.py
@@ -202,14 +202,273 @@
     )(*args)
 
 
-def kinetic(padded):
-    return stencil_scale * (
-        padded[:, :, :-4]
-        - 16.0 * padded[:, :, 1:-3]
-        + 30.0 * padded[:, :, 2:-2]
-        - 16.0 * padded[:, :, 3:-1]
-        + padded[:, :, 4:]
+def exact_dot(a, b, dims=((1,), (0,))):
+    return lax.dot_general(
+        a, b, (dims, ((), ())), precision=highest, preferred_element_type=jnp.float32
     )
+
+
+def full_sum(value):
+    return jnp.sum(jnp.sum(value, axis=0, keepdims=True), axis=1, keepdims=True)
+
+
+def tile_sum(value):
+    return jnp.sum(value.reshape(value.shape[0] // 8, 8, value.shape[1]), axis=0)
+
+
+def combine(scale, real, imag, terms):
+    real, imag = (scale * real, scale * imag)
+    for coef_real, coef_imag, other_real, other_imag in terms:
+        real = real - (coef_real * other_real - coef_imag * other_imag)
+        imag = imag - (coef_real * other_imag + coef_imag * other_real)
+    return (real, imag)
+
+
+def pick(row, k):
+    lane = lax.broadcasted_iota(jnp.int32, row.shape, 1)
+    return jnp.sum(jnp.where(lane == k, row, 0.0), axis=1, keepdims=True)
+
+
+def pack(outer, inner, surface, flags, scalars, ghost_out, first_out, last_out, edge_out):
+    ch_count = ghost_out.shape[0]
+    bs = outer.shape[2]
+    blocks = outer.shape[1] // bs
+    ghost_out[...] = jnp.zeros_like(ghost_out)
+    first_out[...] = jnp.zeros_like(first_out)
+    last_out[...] = jnp.zeros_like(last_out)
+    row_at = lax.broadcasted_iota(jnp.int32, (8, bs), 0)
+    lane_at = lax.broadcasted_iota(jnp.int32, (8, bs), 1)
+    wanted = jnp.where(row_at < 2, row_at, jnp.where(row_at < 4, row_at + bs - 4, -1))
+    select = (lane_at == wanted).astype(jnp.float32)
+    for x in range(2):
+        for b in range(blocks):
+            rows = exact_dot(select, outer[x, b * bs : (b + 1) * bs, :], ((1,), (1,)))
+            for pt in range(2):
+                at = pt * blocks + b
+                first_out[x, at : at + 1, :] = rows[pt : pt + 1]
+                last_out[x, at : at + 1, :] = rows[pt + 2 : pt + 3]
+    edge_out[...] = first_out[...] * flags[0]
+    for layer in range(2):
+        sums = exact_dot(inner, surface[layer])
+        for x in range(2):
+            for p in range(ch_count):
+                for b in range(blocks):
+                    at, start = (layer * blocks + b, (p * blocks + b) * bs)
+                    ghost_out[p, x, at : at + 1, :] = sums[x : x + 1, start : start + bs]
+    put_scalars(scalars, ghost_out, 2 * blocks)
+
+
+def put_scalars(scalars, ghost_out, at):
+    lane = lax.broadcasted_iota(jnp.int32, (1, 128), 1)
+    row = jnp.zeros((1, 128), jnp.float32)
+    for k, value in enumerate(scalars):
+        row = jnp.where(lane == k, value, row)
+    for p in range(ghost_out.shape[0]):
+        ghost_out[p, 0, at : at + 1, :] = row
+
+
+def prepare_kernel(flags, outer, inner, surface, ghost_out, first_out, last_out, edge_out):
+    value = full_sum(inner[...] * inner[...])
+    for x in range(2):
+        part = outer[x]
+        value = value + full_sum(tile_sum(part * part))
+    pack(outer, inner[...], surface, flags, [value], ghost_out, first_out, last_out, edge_out)
+
+
+def step_kernel(column, last_step, *refs):
+    refs = list(refs)
+    take = lambda count: [refs.pop(0) for _ in range(count)]
+    cols, flags, factor, coef, surface, energies = take(6)
+    outer, inner, sums, edges, before, after, full = take(7)
+    olds_sums = take(column)
+    old_outer, old_inner = (take(column), take(column))
+    old_image, old_image_inner = (take(column), take(column))
+    old_ghost, old_edge = (take(column), take(column))
+    if column:
+        new_outer, new_inner, new_ghost, new_edge = take(4)
+    else:
+        new_outer, new_inner, new_ghost, new_edge = (outer, inner, sums, edges)
+    image, image_inner, applied, applied_inner = take(4)
+    if last_step:
+        (ghost_out,) = take(1)
+    else:
+        ghost_out, first_out, last_out, edge_out = take(4)
+    mixed = take(1)[0]
+    bs = outer.shape[2]
+    blocks = outer.shape[1] // bs
+    slots = coef.shape[1]
+    ch_count = edges.shape[0]
+    at_row = 2 * blocks
+
+    terms = []
+    inverse = None
+    if column:
+        history = [ref[0, at_row : at_row + 1, :] for ref in olds_sums]
+        history.append(sums[0, at_row : at_row + 1, :])
+        roots = [lax.rsqrt(pick(history[0], 0) + 1e-06)]
+        for k in range(1, column):
+            roots.append(lax.rsqrt(pick(history[k + 1], 2 * k + 2) + 1e-06))
+        inverse = roots[column - 1]
+        for row in range(column):
+            scale = roots[row] * roots[row] * inverse
+            terms.append(
+                (pick(history[column], 2 * row) * scale, pick(history[column], 2 * row + 1) * scale)
+            )
+
+    def advance(real, imag, others):
+        return combine(
+            inverse, real, imag, [t + o for t, o in zip(terms, others)]
+        )
+
+    if column:
+        real, imag = advance(sums[0], sums[1], [(o[0], o[1]) for o in old_ghost])
+        new_ghost[0] = real
+        new_ghost[1] = imag
+        for p in range(ch_count):
+            real, imag = advance(edges[p, 0], edges[p, 1], [(o[p, 0], o[p, 1]) for o in old_edge])
+            new_edge[p, 0] = real
+            new_edge[p, 1] = imag
+        real, imag = advance(
+            inner[0:1], inner[1:2], [(o[0:1], o[1:2]) for o in old_inner]
+        )
+        new_inner[0:1] = real
+        new_inner[1:2] = imag
+        real, imag = advance(
+            energies[...] * inner[0:1],
+            energies[...] * inner[1:2],
+            [(o[0:1], o[1:2]) for o in old_image_inner],
+        )
+        image_inner[0:1] = real
+        image_inner[1:2] = imag
+    else:
+        image_inner[...] = energies[...] * inner[...]
+
+    mixed[...] = jnp.zeros_like(mixed)
+    for p in range(ch_count):
+        for x in range(2):
+            for b in range(blocks):
+                start = (p * blocks + b) * bs
+                zero = new_edge[p, x, b : b + 1, :]
+                one = new_edge[p, x, blocks + b : blocks + b + 1, :]
+                mixed[0, x : x + 1, start : start + bs] = -16.0 * zero + one
+                mixed[1, x : x + 1, start : start + bs] = zero
+    added = exact_dot(mixed[0], surface[0], ((1,), (1,)))
+    added = added + exact_dot(mixed[1], surface[1], ((1,), (1,)))
+    applied_inner[...] = image_inner[...] + stencil_scale * added[0:2]
+
+    row_at = lax.broadcasted_iota(jnp.int32, (8, bs), 0)
+    lane_at = lax.broadcasted_iota(jnp.int32, (8, bs), 1)
+
+    def weight(row, lane, value):
+        return jnp.where((row_at == row) & (lane_at == lane), value * stencil_scale, 0.0)
+
+    weights = (
+        weight(0, 0, 1.0)
+        + weight(1, 0, -16.0)
+        + weight(1, 1, 1.0)
+        + weight(2, bs - 1, -16.0)
+        + weight(2, bs - 2, 1.0)
+        + weight(3, bs - 1, 1.0)
+    )
+    zeros = jnp.zeros((4, bs), jnp.float32)
+    lane = lax.broadcasted_iota(jnp.int32, (bs, bs), 1)
+
+    def rim(far, near, next0, next1):
+        rows = jnp.concatenate([far, near, next0, next1, zeros], axis=0)
+        return exact_dot(rows, weights, ((0,), (0,)))
+
+    count = column + 1
+    reals = [jnp.zeros((8, bs), jnp.float32) for _ in range(count)]
+    imags = [jnp.zeros((8, bs), jnp.float32) for _ in range(count)]
+    square = jnp.zeros((8, bs), jnp.float32)
+    for b in range(blocks):
+        rows = slice(b * bs, (b + 1) * bs)
+        product = jnp.zeros((bs, 2 * bs), jnp.float32)
+        for s in range(0, slots, 2):
+            sides = []
+            for t in (s, s + 1):
+                col = cols[b, t]
+                place = pl.ds(pl.multiple_of(lax.rem(col, blocks) * bs, bs), bs)
+                owner = lax.div(col, blocks)
+                scale = factor[b, t : t + 1, :]
+                sides.append(
+                    jnp.concatenate(
+                        [full[owner, 0, place, :] * scale, full[owner, 1, place, :] * scale], axis=1
+                    )
+                )
+            left = jnp.concatenate([coef[b, s], coef[b, s + 1]], axis=1)
+            product = product + exact_dot(left, jnp.concatenate(sides, axis=0))
+        parts = []
+        for x in range(2):
+            value = outer[x, rows, :]
+            m1 = jnp.where(lane >= 1, pltpu.roll(value, 1, 1), 0.0)
+            m2 = jnp.where(lane >= 2, pltpu.roll(value, 2, 1), 0.0)
+            p1 = jnp.where(lane < bs - 1, pltpu.roll(value, bs - 1, 1), 0.0)
+            p2 = jnp.where(lane < bs - 2, pltpu.roll(value, bs - 2, 1), 0.0)
+            stencil = stencil_scale * (m2 - 16.0 * m1 + 30.0 * value - 16.0 * p1 + p2)
+            sides = rim(
+                before[x, b : b + 1, :] * flags[1],
+                before[x, blocks + b : blocks + b + 1, :] * flags[1],
+                after[x, b : b + 1, :] * flags[2],
+                after[x, blocks + b : blocks + b + 1, :] * flags[2],
+            )
+            parts.append(stencil + sides + product[:, x * bs : (x + 1) * bs])
+        vector = [outer[0, rows, :], outer[1, rows, :]]
+        if column:
+            parts = advance(
+                parts[0], parts[1], [(o[0, rows, :], o[1, rows, :]) for o in old_image]
+            )
+            vector = advance(
+                vector[0], vector[1], [(o[0, rows, :], o[1, rows, :]) for o in old_outer]
+            )
+            for x in range(2):
+                new_outer[x, rows, :] = vector[x]
+        result = []
+        none = jnp.zeros((1, bs), jnp.float32)
+        for x in range(2):
+            if not last_step:
+                image[x, rows, :] = parts[x]
+            value = parts[x] + rim(
+                new_ghost[x, blocks + b : blocks + b + 1, :] * flags[0],
+                new_ghost[x, b : b + 1, :] * flags[0],
+                none,
+                none,
+            )
+            if not last_step:
+                applied[x, rows, :] = value
+            result.append(value)
+        for k in range(count):
+            if k < column:
+                own = [old_outer[k][x, rows, :] for x in range(2)]
+            else:
+                own = vector
+            reals[k] = reals[k] + tile_sum(own[0] * result[0] + own[1] * result[1])
+            imags[k] = imags[k] + tile_sum(own[0] * result[1] - own[1] * result[0])
+        square = square + tile_sum(vector[0] * vector[0] + vector[1] * vector[1])
+
+    scalars = []
+    w_real, w_imag = (applied_inner[0:1], applied_inner[1:2])
+    for k in range(count):
+        ref = old_inner[k] if k < column else new_inner
+        u_real, u_imag = (ref[0:1], ref[1:2])
+        scalars.append(full_sum(reals[k]) + full_sum(u_real * w_real + u_imag * w_imag))
+        scalars.append(full_sum(imags[k]) + full_sum(u_real * w_imag - u_imag * w_real))
+    scalars.append(full_sum(square) + full_sum(new_inner[...] * new_inner[...]))
+    if last_step:
+        ghost_out[...] = jnp.zeros_like(ghost_out)
+        put_scalars(scalars, ghost_out, at_row)
+    else:
+        pack(
+            applied,
+            applied_inner[...],
+            surface,
+            flags,
+            scalars,
+            ghost_out,
+            first_out,
+            last_out,
+            edge_out,
+        )
 
 
 def propagate(hess):
@@ -231,14 +490,6 @@
     for repeat in range(squarings):
         series = jnp.dot(series, series, precision=highest)
     return (series[:ITERS, 0], series[ITERS:, 0])
-
-
-def combine(scale, vector, terms):
-    real, imag = (scale * vector[0], scale * vector[1])
-    for (coef_real, coef_imag), other in terms:
-        real = real - (coef_real * other[0] - coef_imag * other[1])
-        imag = imag - (coef_real * other[1] + coef_imag * other[0])
-    return jnp.stack([real, imag])
 
 
 def per_device(
@@ -264,127 +515,100 @@
     radius = inner_radius + (positions + 1).astype(jnp.float32) * grid_step
     first_sector = (sec_index == 0).astype(jnp.float32)
     last_sector = (sec_index == lax.axis_size("sec") - 1).astype(jnp.float32)
-    pair_rows = 4 * ch_dev // 128
-    side_rows = (pair_rows // 8 + 1) * 8
     local_cols = lax.dynamic_slice_in_dim(block_cols, ch_index * rows_dev, rows_dev, 0)
     local_kind = lax.dynamic_slice_in_dim(block_kind, ch_index * rows_dev, rows_dev, 0)
     local_polar = lax.dynamic_slice_in_dim(polarisation, ch_index * rows_dev, rows_dev, 0)
     local_factor = radial_factor(local_kind, local_polar, laser_field, radius)
-    lane = lax.broadcasted_iota(jnp.int32, (1, 1, rad_dev), 2)
-
-    def padded_rows(value, count):
-        return jnp.concatenate([value, jnp.zeros((count - value.shape[0], 128), jnp.float32)], axis=0)
-
-    def column_rows(outer, start):
-        pair = jnp.stack([outer[:, :, start], outer[:, :, start + 1]], axis=1)
-        return padded_rows(pair.reshape(pair_rows, 128), side_rows)
-
-    def side_columns(rows, keep):
-        pair = rows[:pair_rows].reshape(2, 2, ch_dev) * keep
-        return jnp.transpose(pair, (0, 2, 1))
-
-    def scalar_row(scalars):
-        place = lax.broadcasted_iota(jnp.int32, (1, 128), 1)
-        row = jnp.zeros((1, 128), jnp.float32)
-        for k, value in enumerate(scalars):
-            row = jnp.where(place == k, value, row)
-        return row
-
-    def exchanged(vector, scalars):
-        outer, inner = vector
-        partial_sum = jnp.einsum("xk,lkc->xlc", inner, surface, precision=highest)
-        sliced = jnp.transpose(partial_sum.reshape(2, 2, ch_count, ch_dev), (2, 0, 1, 3))
-        sliced = sliced.reshape(ch_count, pair_rows, 128)
-        tail = padded_rows(scalar_row(scalars), side_rows - pair_rows)
-        tail = jnp.broadcast_to(tail[None], (ch_count,) + tail.shape)
-        first = column_rows(outer, 0)
-        last = column_rows(outer, rad_dev - 2)
-        sums, edge_rows, before, after, full = exchange(
-            dims, jnp.concatenate([sliced, tail], axis=1), first * first_sector, first, last, outer
-        )
-        ghosts = sums[:pair_rows].reshape(2, 2, ch_dev)
-        edges = edge_rows[:, :pair_rows].reshape(ch_count, 2, 2, ch_dev)
-        edges = jnp.transpose(edges, (1, 2, 0, 3)).reshape(2, 2, ch_count * ch_dev)
-        grouped = full.reshape(ch_count, 2, rows_dev, block_size, rad_dev)
-        picked = grouped[local_cols // rows_dev, :, local_cols % rows_dev]
-        product = jnp.einsum("lsab,lsxbr->xlsar", coefficients, picked, precision=highest)
-        padded = jnp.concatenate(
-            [side_columns(before, 1.0 - first_sector), outer, side_columns(after, 1.0 - last_sector)],
-            axis=2,
-        )
-        image = kinetic(padded) + jnp.sum(
-            product * local_factor[None, :, :, None, :], axis=2
-        ).reshape(2, ch_dev, rad_dev)
-        return (ghosts, edges, sums[pair_rows], (image, energies * inner))
-
-    def with_boundary(image, ghosts, edges):
-        outer, inner = image
-        at_zero = (-16.0 * ghosts[:, 0] + ghosts[:, 1]) * (stencil_scale * first_sector)
-        at_one = ghosts[:, 0] * (stencil_scale * first_sector)
-        rim = jnp.where(
-            lane == 0, at_zero[:, :, None], jnp.where(lane == 1, at_one[:, :, None], 0.0)
-        )
-        mixed = jnp.stack([-16.0 * edges[:, 0] + edges[:, 1], edges[:, 0]], axis=1)
-        inner_add = jnp.einsum("xlc,lkc->xk", mixed, surface, precision=highest)
-        return (outer + rim, inner + stencil_scale * inner_add)
-
-    def norm_of(vector):
-        return jnp.sum(vector[0] * vector[0]) + jnp.sum(vector[1] * vector[1])
-
-    def product_of(a, b):
-        real = jnp.sum(a[0] * b[0]) + jnp.sum(a[1] * b[1])
-        imag = jnp.sum(a[0][0] * b[0][1] - a[0][1] * b[0][0]) + jnp.sum(
-            a[1][0] * b[1][1] - a[1][1] * b[1][0]
-        )
-        return [real, imag]
-
-    current = (outer_wave, inner_wave)
-    ghosts, edges, totals, image = exchanged(current, [norm_of(current)])
-    norms = [jnp.sqrt(totals[0] + 1e-06)]
-    basis, images, rims = [current], [image], [(ghosts, edges)]
+    flags = jnp.stack([first_sector, 1.0 - first_sector, 1.0 - last_sector])
+    shape = functools.partial(jax.ShapeDtypeStruct, dtype=jnp.float32)
+    vmem = pl.BlockSpec(memory_space=pltpu.VMEM)
+    smem = pl.BlockSpec(memory_space=pltpu.SMEM)
+    params = pltpu.CompilerParams(vmem_limit_bytes=56 * 1024 * 1024)
+    side = shape((2, 8, 128))
+    packed = [shape((ch_count, 2, 8, 128)), side, side, side]
+    outer_shape, inner_shape = (shape(outer_wave.shape), shape(inner_wave.shape))
+
+    def swap(vector, payload):
+        ghost_part, first, last, edge = [value.reshape(-1, 16, 128) for value in payload]
+        sums, edges, before, after, full = exchange(
+            dims, ghost_part, edge[0], first[0], last[0], vector
+        )
+        return (
+            sums.reshape(2, 8, 128),
+            edges.reshape(ch_count, 2, 8, 128),
+            before.reshape(2, 8, 128),
+            after.reshape(2, 8, 128),
+            full,
+        )
+
+    payload = pl.pallas_call(
+        prepare_kernel,
+        out_shape=packed,
+        in_specs=[smem] + [vmem] * 3,
+        out_specs=[vmem] * 4,
+        compiler_params=params,
+        name="prepare",
+    )(flags, outer_wave, inner_wave, surface)
+    applied, applied_inner = (outer_wave, inner_wave)
+    history, outers, inners, images, image_inners, ghosts, rims = ([], [], [], [], [], [], [])
+    for column in range(ITERS):
+        last_step = column + 1 == ITERS
+        sums, edges, before, after, full = swap(applied, payload)
+        args = [local_cols, flags, local_factor, coefficients, surface, energies[None]]
+        args += [applied, applied_inner, sums, edges, before, after, full]
+        args += history + outers + inners + images + image_inners + ghosts + rims
+        outs = []
+        if column:
+            outs += [outer_shape, inner_shape, side, shape((ch_count, 2, 8, 128))]
+        outs += [outer_shape, inner_shape, outer_shape, inner_shape]
+        outs += packed[:1] if last_step else packed
+        results = list(
+            pl.pallas_call(
+                functools.partial(step_kernel, column, last_step),
+                out_shape=outs,
+                in_specs=[smem, smem] + [vmem] * (len(args) - 2),
+                out_specs=[vmem] * len(outs),
+                scratch_shapes=[pltpu.VMEM((2, 8, ch_count * ch_dev), jnp.float32)],
+                compiler_params=params,
+                name="step",
+            )(*args)
+        )
+        if column:
+            new = results[:4]
+            results = results[4:]
+        else:
+            new = [applied, applied_inner, sums, edges]
+        for store, value in zip((outers, inners, ghosts, rims), new):
+            store.append(value)
+        history.append(sums)
+        image, image_inner, applied, applied_inner = results[:4]
+        images.append(image)
+        image_inners.append(image_inner)
+        payload = results[4:]
+    last_rows = payload[0][:, 0]
+    history.append(exchange(dims, last_rows)[0][None])
+    rows = [value[0, 2 * rows_dev] for value in history]
+    norms = [jnp.sqrt(rows[0][0] + 1e-06)]
     hess = {}
     for column in range(ITERS):
-        applied = with_boundary(images[column], *rims[column])
-        scalars = []
-        for vector in basis:
-            scalars += product_of(vector, applied)
-        scalars.append(norm_of(basis[column]))
-        if column + 1 < ITERS:
-            ghosts, edges, totals, applied_image = exchanged(applied, scalars)
-        else:
-            row = padded_rows(scalar_row(scalars), 8)
-            totals = exchange(dims, jnp.broadcast_to(row[None], (ch_count, 8, 128)))[0][0]
+        totals = rows[column + 1]
         if column:
             norms.append(jnp.sqrt(totals[2 * column + 2] + 1e-06))
             hess[column, column - 1] = (norms[column], jnp.zeros((), jnp.float32))
-        terms = []
         for row in range(column + 1):
             scale = 1.0 / (norms[row] * norms[column])
-            real, imag = (totals[2 * row] * scale, totals[2 * row + 1] * scale)
-            hess[row, column] = (real, imag)
-            terms.append((real / norms[row], imag / norms[row]))
-        if column + 1 < ITERS:
-            inverse = 1.0 / norms[column]
-
-            def advance(new, olds):
-                return combine(inverse, new, list(zip(terms, olds)))
-
-            basis.append(
-                tuple(advance(applied[k], [old[k] for old in basis]) for k in range(2))
-            )
-            images.append(
-                tuple(advance(applied_image[k], [old[k] for old in images]) for k in range(2))
-            )
-            new_rim = (ghosts, edges)
-            rims.append(tuple(advance(new_rim[k], [old[k] for old in rims]) for k in range(2)))
+            hess[row, column] = (totals[2 * row] * scale, totals[2 * row + 1] * scale)
     coef_real, coef_imag = propagate(hess)
     outputs = []
-    for k in range(2):
-        terms = []
+    for store in (outers, inners):
+        real, imag = (0.0, 0.0)
         for column in range(ITERS):
             scale = norms[0] / norms[column]
-            terms.append(((-coef_real[column] * scale, -coef_imag[column] * scale), basis[column][k]))
-        outputs.append(combine(0.0, basis[0][k], terms))
+            part_real, part_imag = (coef_real[column] * scale, coef_imag[column] * scale)
+            value = store[column]
+            real = real + (part_real * value[0] - part_imag * value[1])
+            imag = imag + (part_real * value[1] + part_imag * value[0])
+        outputs.append(jnp.stack([real, imag]))
     return tuple(outputs)
 
 

time: 452 us -> 228 us (0.50)
  local copies, waits for them, and re-layouts: 105 us -> 11.3 us
  other arithmetic: 82.3 us -> 5.47 us
  matrix products: 51.2 us -> 2.35 us
  Pallas kernels: 154 us -> 186 us
  between operations: 53.8 us -> 21.8 us
    dot_general x12 -> x0, matrix products: 48.9 us -> none  [the longest x4 32.9 us: exchanged(): jnp.einsum('lsab,lsxbr->xlsar', coefficients, picked, precision=highest)]
    pallas_call x0 -> x5, Pallas kernels: none -> 32.1 us  [the longest x4 29.2 us: per_device(): pl.pallas_call(functools.partial(step_kernel, column, last_step), out_sha...]
    reduce_sum x15 -> x0, other arithmetic: 26.8 us -> none  [the longest x5 8.57 us: product_of(): jnp.sum(a[0][0] * b[0][1] - a[0][1] * b[0][0])]
    reshape x30 -> x0, local copies, waits for them, and re-layouts: 25.8 us -> none  [the longest x8 7.78 us: column_rows(): return padded_rows(pair.reshape(pair_rows, 128), side_rows)]
    sub x26 -> x0, other arithmetic: 22.7 us -> none  [the longest x22 21.2 us: combine(): real = real - (coef_real * other[0] - coef_imag * other[1])]
    mul x16 -> x0, local copies, waits for them, and re-layouts: 19.4 us -> none  [side_columns(): pair = rows[:pair_rows].reshape(2, 2, ch_dev) * keep]
    gather x4 -> x0, local copies, waits for them, and re-layouts: 15.6 us -> none  [exchanged(): picked = grouped[local_cols // rows_dev, :, local_cols % rows_dev]]
    mul x14 -> x0, other arithmetic: 9.72 us -> none  [the longest x7 7.76 us: side_columns(): pair = rows[:pair_rows].reshape(2, 2, ch_dev) * keep]
where the time goes in v3:
time: 228 us; the launch traced here: 227 us
  Pallas kernels  186 us (82%)
  between operations  21.8 us (10%)
  local copies, waits for them, and re-layouts  11.3 us (5%)
  other arithmetic  5.47 us (2%)
  matrix products  2.35 us (1%)
    pallas_call x5, Pallas kernels, exchange(): pl.pallas_call(functools.partial(exchange_kernel, dims, bulk), out_shape=...  154 us
    pallas_call x4, Pallas kernels, per_device(): pl.pallas_call(functools.partial(step_kernel, column, last_step), out_sha...  29.2 us
    slice x4, local copies, waits for them, and re-layouts, per_device(): hess[row, column] = (totals[2 * row] * scale, totals[2 * row + 1] * scale)  6.21 us

profile of v3, /device:TPU:1, one launch (start us, length us, event | category | flops | bytes accessed | tf_op | source)
XLA Modules:
  0.0 226.7 jit_solution(9237514397411724554)
XLA Ops:
  0.6 0.8 constant_dynamic-slice_fusion
  1.4 0.7 copy.47.refs_0_
  2.1 0.6 pad_maximum_fusion.2.flags.refs_1_
  2.8 0.7 select_reduce_fusion
  3.5 0.8 dynamic-slice_compare_fusion.1
  4.5 0.7 select_select_fusion.refs_2_
  5.1 2.9 %prepare.1 = (f32[4,2,8,128]{3,2,1,0:T(8,128)}, f32[2,8,128]{2,1,0:T(8,128)}, f32[2,8,128]{2,1,0:T(8,128)}, f32[2,8,128]{2,1,0:T(8,128)}) custom-call(f32[3]{0:T(128)} %pad_maximum_fusion.2.flags.refs_1_, f32[2,384,128]{2,1,0:T(8,128)} %refs_16_.1, f32[2,64]{1,0:T(2,128)} %refs_19_.1, f32[2,64,1536]{2,1,0:T(8,128)} %refs_4_.9), custom_call_target="tpu_custom_call" | custom-call | tf_op jit(solution)/shard_map/prepare/pallas_call | solution.py:544
  8.1 41.7 %exchange_bulk.4 = (f32[16,128]{1,0:T(8,128)}, f32[4,16,128]{2,1,0:T(8,128)}, f32[16,128]{1,0:T(8,128)}, f32[16,128]{1,0:T(8,128)}, f32[4,2,384,128]{3,2,1,0:T(8,128)}) custom-call(f32[4,16,128]{2,1,0:T(8,128)} %bitcast.131, f32[16,128]{1,0:T(8,128)} %bitcast.155, f32[16,128]{1,0:T(8,128)} %bitcast.153, f32[16,128]{1,0:T(8,128)} %bitcast.154, ...), custom_call_target="tpu_custom_call" | custom-call | tf_op jit(solution)/shard_map/exchange_bulk/pallas_call | solution.py:194
  49.8 6.9 %step.4 = (f32[2,384,128]{2,1,0:T(8,128)}, f32[2,64]{1,0:T(2,128)}, f32[2,384,128]{2,1,0:T(8,128)}, f32[2,64]{1,0:T(2,128)}, f32[4,2,8,128]{3,2,1,0:T(8,128)}, /...) custom-call(s32[3,8]{1,0:T(4,128)} %copy.47.refs_0_, f32[3]{0:T(128)} %pad_maximum_fusion.2.flags.refs_1_, ...), custom_call_target="tpu_custom_call" | custom-call | tf_op jit(solution)/shard_map/step/pallas_call | solution.py:566
  56.7 29.5 %exchange_bulk.5 = (f32[16,128]{1,0:T(8,128)}, f32[4,16,128]{2,1,0:T(8,128)}, f32[16,128]{1,0:T(8,128)}, f32[16,128]{1,0:T(8,128)}, f32[4,2,384,128]{3,2,1,0:T(8,128)}) custom-call(f32[4,16,128]{2,1,0:T(8,128)} %bitcast.130, f32[16,128]{1,0:T(8,128)} %bitcast.152, f32[16,128]{1,0:T(8,128)} %bitcast.150, f32[16,128]{1,0:T(8,128)} %bitcast.151, ...), custom_call_target="tpu_custom_call" | custom-call | tf_op jit(solution)/shard_map/exchange_bulk/pallas_call | solution.py:194
  86.2 7.2 %step.5 = (f32[2,384,128]{2,1,0:T(8,128)}, f32[2,64]{1,0:T(2,128)}, f32[2,8,128]{2,1,0:T(8,128)}, f32[4,2,8,128]{3,2,1,0:T(8,128)}, f32[2,384,128]{2,1,0:T(8,128...) custom-call(s32[3,8]{1,0:T(4,128)} %copy.47.refs_0_, ...), custom_call_target="tpu_custom_call" | custom-call | tf_op jit(solution)/shard_map/step/pallas_call | solution.py:566
  93.4 33.6 %exchange_bulk.6 = (f32[16,128]{1,0:T(8,128)}, f32[4,16,128]{2,1,0:T(8,128)}, f32[16,128]{1,0:T(8,128)}, f32[16,128]{1,0:T(8,128)}, f32[4,2,384,128]{3,2,1,0:T(8,128)}) custom-call(f32[4,16,128]{2,1,0:T(8,128)} %bitcast.128, f32[16,128]{1,0:T(8,128)} %bitcast.144, f32[16,128]{1,0:T(8,128)} %bitcast.142, f32[16,128]{1,0:T(8,128)} %bitcast.143, ...), custom_call_target="tpu_custom_call" | custom-call | tf_op jit(solution)/shard_map/exchange_bulk/pallas_call | solution.py:194
  127.0 7.8 %step.6 = (f32[2,384,128]{2,1,0:T(8,128)}, f32[2,64]{1,0:T(2,128)}, f32[2,8,128]{2,1,0:T(8,128)}, f32[4,2,8,128]{3,2,1,0:T(8,128)}, f32[2,384,128]{2,1,0:T(8,128...) custom-call(s32[3,8]{1,0:T(4,128)} %copy.47.refs_0_, ...), custom_call_target="tpu_custom_call" | custom-call | tf_op jit(solution)/shard_map/step/pallas_call | solution.py:566
  134.8 30.4 %exchange_bulk.7 = (f32[16,128]{1,0:T(8,128)}, f32[4,16,128]{2,1,0:T(8,128)}, f32[16,128]{1,0:T(8,128)}, f32[16,128]{1,0:T(8,128)}, f32[4,2,384,128]{3,2,1,0:T(8,128)}) custom-call(f32[4,16,128]{2,1,0:T(8,128)} %bitcast.129, f32[16,128]{1,0:T(8,128)} %bitcast.147, f32[16,128]{1,0:T(8,128)} %bitcast.145, f32[16,128]{1,0:T(8,128)} %bitcast.146, ...), custom_call_target="tpu_custom_call" | custom-call | tf_op jit(solution)/shard_map/exchange_bulk/pallas_call | solution.py:194
  165.5 7.3 %step.7 = (f32[2,384,128]{2,1,0:T(8,128)}, f32[2,64]{1,0:T(2,128)}, f32[2,8,128]{2,1,0:T(8,128)}, f32[4,2,8,128]{3,2,1,0:T(8,128)}, f32[2,384,128]{2,1,0:T(8,128...) custom-call(s32[3,8]{1,0:T(4,128)} %copy.47.refs_0_, ...), custom_call_target="tpu_custom_call" | custom-call | tf_op jit(solution)/shard_map/step/pallas_call | solution.py:566
  172.8 1.4 slice_bitcast_fusion.refs_0_
  174.2 18.4 %exchange_sums.1 = f32[8,128]{1,0:T(8,128)} custom-call(f32[4,8,128]{2,1,0:T(8,128)} %slice_bitcast_fusion.refs_0_), custom_call_target="tpu_custom_call" | custom-call | tf_op jit(solution)/shard_map/exchange_sums/pallas_call | solution.py:194
  192.6 1.7 fusion.14
  196.3 1.6 fusion.12
  199.9 1.5 fusion.11
  203.4 1.2 slice.292
  212.9 1.4 fusion.10
  216.1 0.1 fusion.7
  216.3 0.1 fusion.6
  216.4 0.1 fusion.5
  216.6 0.1 fusion.4
  216.7 0.1 fusion.3
  216.9 0.1 fusion.2
  218.2 0.6 fusion.13
  224.0 1.1 add_add_fusion
  225.3 0.8 pad_maximum_fusion
  226.1 0.6 pad_maximum_fusion.1
  (82 shorter events, 2.2 us)
Async XLA Ops:
  165.2 50.4 %copy-start.7 = (f32[8,8]{1,0:T(8,128)S(1)}, f32[8,8]{1,0:T(8,128)}, u32[]{:S(2)}) copy-start(f32[8,8]{1,0:T(8,128)} %constant.163.clone) | copy-start | bytes 772
  165.2 50.4 %copy-start.8 = (f32[8,8]{1,0:T(8,128)S(1)}, f32[8,8]{1,0:T(8,128)}, u32[]{:S(2)}) copy-start(f32[8,8]{1,0:T(8,128)} %constant.162.clone) | copy-start | bytes 772
  165.2 50.4 %copy-start.9 = (f32[8,8]{1,0:T(8,128)S(1)}, f32[8,8]{1,0:T(8,128)}, u32[]{:S(2)}) copy-start(f32[8,8]{1,0:T(8,128)} %constant.161.clone) | copy-start | bytes 772
  165.2 50.4 %copy-start.10 = (f32[8,8]{1,0:T(8,128)S(1)}, f32[8,8]{1,0:T(8,128)}, u32[]{:S(2)}) copy-start(f32[8,8]{1,0:T(8,128)} %constant.160.clone) | copy-start | bytes 772
  165.3 50.4 %copy-start.11 = (f32[8,8]{1,0:T(8,128)S(1)}, f32[8,8]{1,0:T(8,128)}, u32[]{:S(2)}) copy-start(f32[8,8]{1,0:T(8,128)} %constant.159.clone) | copy-start | bytes 772
  165.3 50.4 %copy-start.12 = (f32[8,8]{1,0:T(8,128)S(1)}, f32[8,8]{1,0:T(8,128)}, u32[]{:S(2)}) copy-start(f32[8,8]{1,0:T(8,128)} %constant.158.clone) | copy-start | bytes 772
  165.3 50.4 %copy-start.13 = (f32[8,8]{1,0:T(8,128)S(1)}, f32[8,8]{1,0:T(8,128)}, u32[]{:S(2)}) copy-start(f32[8,8]{1,0:T(8,128)} %constant.157.clone) | copy-start | bytes 772
  165.3 50.4 %copy-start.14 = (f32[8,8]{1,0:T(8,128)S(1)}, f32[8,8]{1,0:T(8,128)}, u32[]{:S(2)}) copy-start(f32[8,8]{1,0:T(8,128)} %constant.156.clone) | copy-start | bytes 772
  165.3 50.4 %copy-start.15 = (f32[8,8]{1,0:T(8,128)S(1)}, f32[8,8]{1,0:T(8,128)}, u32[]{:S(2)}) copy-start(f32[8,8]{1,0:T(8,128)} %constant.155.clone) | copy-start | bytes 772
  165.3 50.4 %copy-start.16 = (f32[8,8]{1,0:T(8,128)S(1)}, f32[8,8]{1,0:T(8,128)}, u32[]{:S(2)}) copy-start(f32[8,8]{1,0:T(8,128)} %constant.153.clone) | copy-start | bytes 772
  165.3 50.4 %copy-start.17 = (f32[8,8]{1,0:T(8,128)S(1)}, f32[8,8]{1,0:T(8,128)}, u32[]{:S(2)}) copy-start(f32[8,8]{1,0:T(8,128)} %constant.152.clone) | copy-start | bytes 772
  165.3 50.4 %copy-start.18 = (f32[8,8]{1,0:T(8,128)S(1)}, f32[8,8]{1,0:T(8,128)}, u32[]{:S(2)}) copy-start(f32[8,8]{1,0:T(8,128)} %constant.151.clone) | copy-start | bytes 772
  165.4 50.4 %copy-start.19 = (f32[8,8]{1,0:T(8,128)S(1)}, f32[8,8]{1,0:T(8,128)}, u32[]{:S(2)}) copy-start(f32[8,8]{1,0:T(8,128)} %constant.150.clone) | copy-start | bytes 772
  165.4 50.4 %copy-start.20 = (f32[8,8]{1,0:T(8,128)S(1)}, f32[8,8]{1,0:T(8,128)}, u32[]{:S(2)}) copy-start(f32[8,8]{1,0:T(8,128)} %constant.149.clone) | copy-start | bytes 772
  165.4 50.4 %copy-start.21 = (f32[8,8]{1,0:T(8,128)S(1)}, f32[8,8]{1,0:T(8,128)}, u32[]{:S(2)}) copy-start(f32[8,8]{1,0:T(8,128)} %constant.148.clone) | copy-start | bytes 772
  165.4 50.4 %copy-start.22 = (f32[8,8]{1,0:T(8,128)S(1)}, f32[8,8]{1,0:T(8,128)}, u32[]{:S(2)}) copy-start(f32[8,8]{1,0:T(8,128)} %constant.147.clone) | copy-start | bytes 772
  165.4 50.3 %copy-start.23 = (f32[8,8]{1,0:T(8,128)S(1)}, f32[8,8]{1,0:T(8,128)}, u32[]{:S(2)}) copy-start(f32[8,8]{1,0:T(8,128)} %constant.145.clone) | copy-start | bytes 772
  165.4 50.3 %copy-start.24 = (f32[8,8]{1,0:T(8,128)S(1)}, f32[8,8]{1,0:T(8,128)}, u32[]{:S(2)}) copy-start(f32[8,8]{1,0:T(8,128)} %constant.144.clone) | copy-start | bytes 772
  165.4 50.3 %copy-start.25 = (f32[8,8]{1,0:T(8,128)S(1)}, f32[8,8]{1,0:T(8,128)}, u32[]{:S(2)}) copy-start(f32[8,8]{1,0:T(8,128)} %constant.143.clone) | copy-start | bytes 772
  165.4 50.3 %copy-start.26 = (f32[8,8]{1,0:T(8,128)S(1)}, f32[8,8]{1,0:T(8,128)}, u32[]{:S(2)}) copy-start(f32[8,8]{1,0:T(8,128)} %constant.142.clone) | copy-start | bytes 772
  165.5 50.3 %copy-start.27 = (f32[8,8]{1,0:T(8,128)S(1)}, f32[8,8]{1,0:T(8,128)}, u32[]{:S(2)}) copy-start(f32[8,8]{1,0:T(8,128)} %constant.141.clone) | copy-start | bytes 772
  165.5 50.3 %copy-start.28 = (f32[8,8]{1,0:T(8,128)S(1)}, f32[8,8]{1,0:T(8,128)}, u32[]{:S(2)}) copy-start(f32[8,8]{1,0:T(8,128)} %constant.139.clone) | copy-start | bytes 772
  165.5 50.3 %copy-start.29 = (f32[8,8]{1,0:T(8,128)S(1)}, f32[8,8]{1,0:T(8,128)}, u32[]{:S(2)}) copy-start(f32[8,8]{1,0:T(8,128)} %constant.138.clone) | copy-start | bytes 772
  165.5 58.5 %copy-start = (f32[2,384,128]{2,1,0:T(8,128)S(1)}, f32[2,384,128]{2,1,0:T(8,128)}, u32[]{:S(2)}) copy-start(f32[2,384,128]{2,1,0:T(8,128)} %refs_16_.1) | copy-start | bytes 1179652
  165.5 58.5 %copy-start.1 = (f32[2,384,128]{2,1,0:T(8,128)S(1)}, f32[2,384,128]{2,1,0:T(8,128)}, u32[]{:S(2)}) copy-start(f32[2,384,128]{2,1,0:T(8,128)} %get-tuple-element.94.refs_16_.refs_17_) | copy-start | bytes 1179652
  165.5 58.5 %copy-start.2 = (f32[2,384,128]{2,1,0:T(8,128)S(1)}, f32[2,384,128]{2,1,0:T(8,128)}, u32[]{:S(2)}) copy-start(f32[2,384,128]{2,1,0:T(8,128)} %get-tuple-element.111.refs_18_) | copy-start | bytes 1179652
  172.8 52.3 %copy-start.3 = (f32[2,384,128]{2,1,0:T(8,128)S(1)}, f32[2,384,128]{2,1,0:T(8,128)}, u32[]{:S(2)}) copy-start(f32[2,384,128]{2,1,0:T(8,128)} %get-tuple-element.118) | copy-start | bytes 1179652
  225.2 0.9 copy-start.4
  225.2 0.9 copy-start.5
  225.2 0.9 copy-start.6
  225.2 0.9 copy-start.30

commit v4 on v3

--- a/solution.py
+++ b/solution.py
@@ -2,7 +2,6 @@
 
 import jax
 import jax.numpy as jnp
-import numpy as np
 from jax import lax
 from jax.experimental import pallas as pl
 from jax.experimental.pallas import tpu as pltpu
@@ -110,8 +109,11 @@
     if bulk:
         later.append(remote(last_in, before_out, side_send.at[0], side_recv.at[0], up))
         later.append(remote(first_in, after_out, side_send.at[1], side_recv.at[1], down))
+        near = []
         for d in range(1, x_size):
-            later.append(
+            if x_size == 4 and d == 2:
+                continue
+            near.append(
                 remote(
                     outer_in, full_out.at[x], bulk_send.at[d - 1], bulk_recv.at[d - 1], x_peer(d)
                 )
@@ -145,6 +147,13 @@
 
     z_slots[z] = stage(c_slots, c, c_size, c_peer, c_send, c_recv)
     y_slots[y] = stage(z_slots, z, z_size, z_peer, z_send, z_recv)
+    if bulk:
+        for copy in near:
+            copy.wait()
+        if x_size == 4:
+            for half, d, sem in ((0, 1, 1), (1, 3, 3)):
+                held = full_out.at[lax.rem(x + x_size - d, x_size), half]
+                later.append(remote(held, held, bulk_send.at[sem], bulk_recv.at[sem], x_peer(d)))
     value = stage(y_slots, y, y_size, y_peer, y_send, y_recv)
     sum_out[...] = value[0:rows]
     if bulk:
@@ -187,9 +196,9 @@
         pltpu.VMEM((y_size, width, lanes), jnp.float32),
     ]
     for size in (x_size, c_size, z_size, y_size):
-        scratch += [dma((size - 1,)), dma((size - 1,))]
-    if bulk:
-        scratch += [dma((x_size - 1,)), dma((x_size - 1,)), dma((2,)), dma((2,))]
+        scratch += [dma((max(size - 1, 1),)), dma((max(size - 1, 1),))]
+    if bulk:
+        scratch += [dma((x_size,)), dma((x_size,)), dma((2,)), dma((2,))]
         scratch += [dma((x_size - 1,)), dma((x_size - 1,)), dma]
     return pl.pallas_call(
         functools.partial(exchange_kernel, dims, bulk),
@@ -471,25 +480,68 @@
         )
 
 
-def propagate(hess):
-    scaled_block = jnp.zeros((2 * ITERS, 2 * ITERS), jnp.float32)
-    for (i, j), (real, imag) in hess.items():
-        for value, places in (
-            (imag, ((i, j, 1.0), (i + ITERS, j + ITERS, 1.0))),
-            (real, ((i, j + ITERS, 1.0), (i + ITERS, j, -1.0))),
-        ):
-            mask = np.zeros((2 * ITERS, 2 * ITERS), np.float32)
-            for a, b, sign in places:
-                mask[a, b] = sign
-            scaled_block = scaled_block + (time_step * value) * mask
-    scaled_block = scaled_block / 2.0**squarings
-    identity = jnp.eye(2 * ITERS, dtype=jnp.float32)
+def small_product(a, b):
+    value = a[:, 0:1] * b[0:1, :]
+    for k in range(1, 2 * ITERS):
+        value = value + a[:, k : k + 1] * b[k : k + 1, :]
+    return value
+
+
+def finish_kernel(at_row, *refs):
+    history = [ref[0, at_row : at_row + 1, :] for ref in refs[:ITERS]]
+    history.append(refs[ITERS][at_row : at_row + 1, :])
+    outers, inners = (refs[ITERS + 1 : 2 * ITERS + 1], refs[2 * ITERS + 1 : 3 * ITERS + 1])
+    outer_out, inner_out = refs[3 * ITERS + 1 :]
+    squares = [pick(history[0], 0) + 1e-06]
+    for k in range(1, ITERS):
+        squares.append(pick(history[k + 1], 2 * k + 2) + 1e-06)
+    roots = [lax.rsqrt(value) for value in squares]
+    row_at = lax.broadcasted_iota(jnp.int32, (2 * ITERS, 128), 0)
+    lane_at = lax.broadcasted_iota(jnp.int32, (2 * ITERS, 128), 1)
+    matrix = jnp.zeros((2 * ITERS, 128), jnp.float32)
+
+    def put(value, i, j):
+        return jnp.where((row_at == i) & (lane_at == j), value, matrix)
+
+    for j in range(ITERS):
+        for i in range(min(j + 2, ITERS)):
+            if i <= j:
+                scale = roots[i] * roots[j] * time_step
+                real = pick(history[j + 1], 2 * i) * scale
+                imag = pick(history[j + 1], 2 * i + 1) * scale
+                matrix = put(imag, i, j)
+                matrix = put(imag, i + ITERS, j + ITERS)
+            else:
+                real = jnp.sqrt(squares[i]) * time_step
+            matrix = put(real, i, j + ITERS)
+            matrix = put(-real, i + ITERS, j)
+    matrix = matrix * (1.0 / 2.0**squarings)
+    identity = jnp.where(row_at == lane_at, 1.0, 0.0)
     series = identity
     for degree in range(taylor_terms, 0, -1):
-        series = identity + jnp.dot(scaled_block, series, precision=highest) / degree
+        series = identity + small_product(matrix, series) * (1.0 / degree)
     for repeat in range(squarings):
-        series = jnp.dot(series, series, precision=highest)
-    return (series[:ITERS, 0], series[ITERS:, 0])
+        series = small_product(series, series)
+    terms = []
+    start_norm = jnp.sqrt(squares[0])
+    for j in range(ITERS):
+        scale = start_norm * roots[j]
+        terms.append((series[j : j + 1, 0:1] * scale, series[j + ITERS : j + ITERS + 1, 0:1] * scale))
+
+    def total(values):
+        real, imag = (0.0, 0.0)
+        for (part_real, part_imag), (value_real, value_imag) in zip(terms, values):
+            real = real + (part_real * value_real - part_imag * value_imag)
+            imag = imag + (part_real * value_imag + part_imag * value_real)
+        return (real, imag)
+
+    inner_out[0:1], inner_out[1:2] = total([(ref[0:1], ref[1:2]) for ref in inners])
+    bs = outer_out.shape[2]
+    for b in range(outer_out.shape[1] // bs):
+        rows = slice(b * bs, (b + 1) * bs)
+        real, imag = total([(ref[0, rows, :], ref[1, rows, :]) for ref in outers])
+        outer_out[0, rows, :] = real
+        outer_out[1, rows, :] = imag
 
 
 def per_device(
@@ -561,7 +613,7 @@
         if column:
             outs += [outer_shape, inner_shape, side, shape((ch_count, 2, 8, 128))]
         outs += [outer_shape, inner_shape, outer_shape, inner_shape]
-        outs += packed[:1] if last_step else packed
+        outs += [shape((ch_count, 1, 8, 128))] if last_step else packed
         results = list(
             pl.pallas_call(
                 functools.partial(step_kernel, column, last_step),
@@ -585,31 +637,18 @@
         images.append(image)
         image_inners.append(image_inner)
         payload = results[4:]
-    last_rows = payload[0][:, 0]
-    history.append(exchange(dims, last_rows)[0][None])
-    rows = [value[0, 2 * rows_dev] for value in history]
-    norms = [jnp.sqrt(rows[0][0] + 1e-06)]
-    hess = {}
-    for column in range(ITERS):
-        totals = rows[column + 1]
-        if column:
-            norms.append(jnp.sqrt(totals[2 * column + 2] + 1e-06))
-            hess[column, column - 1] = (norms[column], jnp.zeros((), jnp.float32))
-        for row in range(column + 1):
-            scale = 1.0 / (norms[row] * norms[column])
-            hess[row, column] = (totals[2 * row] * scale, totals[2 * row + 1] * scale)
-    coef_real, coef_imag = propagate(hess)
-    outputs = []
-    for store in (outers, inners):
-        real, imag = (0.0, 0.0)
-        for column in range(ITERS):
-            scale = norms[0] / norms[column]
-            part_real, part_imag = (coef_real[column] * scale, coef_imag[column] * scale)
-            value = store[column]
-            real = real + (part_real * value[0] - part_imag * value[1])
-            imag = imag + (part_real * value[1] + part_imag * value[0])
-        outputs.append(jnp.stack([real, imag]))
-    return tuple(outputs)
+    last_sums = exchange(dims, payload[0].reshape(ch_count, 8, 128))[0]
+    args = history + [last_sums] + outers + inners
+    return tuple(
+        pl.pallas_call(
+            functools.partial(finish_kernel, 2 * rows_dev),
+            out_shape=[outer_shape, inner_shape],
+            in_specs=[vmem] * len(args),
+            out_specs=[vmem] * 2,
+            compiler_params=params,
+            name="finish",
+        )(*args)
+    )
 
 
 def solution(mesh):

time: 228 us -> 178 us (0.78)
  between operations: 21.8 us -> 0.71 us
  Pallas kernels: 186 us -> 172 us
  local copies, waits for them, and re-layouts: 11.3 us -> 1.7 us
  other arithmetic: 5.47 us -> 2.8 us
  matrix products: 2.35 us -> 0 us
    pallas_call x5, Pallas kernels: 154 us -> 137 us  [exchange(): pl.pallas_call(functools.partial(exchange_kernel, dims, bulk), out_shape=...]
    slice x6 -> x0, local copies, waits for them, and re-layouts: 8.07 us -> none  [the longest x4 6.21 us: per_device(): hess[row, column] = (totals[2 * row] * scale, totals[2 * row + 1] * scale)]
    pallas_call x0 -> x1, Pallas kernels: none -> 3.42 us  [per_device(): pl.pallas_call(functools.partial(finish_kernel, 2 * rows_dev), out_shape=...]
    dot_general x17 -> x0, matrix products: 2.35 us -> none  [the longest x10 1.38 us: propagate(): jnp.dot(scaled_block, series, precision=highest) / degree]
where the time goes in v4:
time: 178 us; the launch traced here: 177 us
  Pallas kernels  172 us (97%)
  other arithmetic  2.8 us (2%)
    pallas_call x5, Pallas kernels, exchange(): pl.pallas_call(functools.partial(exchange_kernel, dims, bulk), out_shape=...  137 us
    pallas_call x4, Pallas kernels, per_device(): pl.pallas_call(functools.partial(step_kernel, column, last_step), out_sha...  29 us

profile of v4, /device:TPU:1, one launch (start us, length us, event | category | flops | bytes accessed | tf_op | source)
XLA Modules:
  0.0 177.3 jit_solution(14839401164360744905)
XLA Ops:
  0.6 0.6 pad_maximum_fusion.flags.refs_1_
  1.3 0.8 dynamic-slice_compare_fusion.1
  2.0 0.1 copy.16
  2.1 0.1 copy.17
  2.2 0.8 constant_dynamic-slice_fusion
  3.0 0.1 copy.18
  3.1 0.7 select_reduce_fusion
  3.8 0.6 copy.19.refs_0_
  4.5 0.7 select_select_fusion.refs_2_
  5.2 2.9 %prepare.1 = (f32[4,2,8,128]{3,2,1,0:T(8,128)}, f32[2,8,128]{2,1,0:T(8,128)}, f32[2,8,128]{2,1,0:T(8,128)}, f32[2,8,128]{2,1,0:T(8,128)}) custom-call(f32[3]{0:T(128)} %pad_maximum_fusion.flags.refs_1_, f32[2,384,128]{2,1,0:T(8,128)} %refs_5_.1, f32[2,64]{1,0:T(2,128)} %refs_9_.1, f32[2,64,1536]{2,1,0:T(8,128)} %refs_4_.9), custom_call_target="tpu_custom_call" | custom-call | tf_op jit(solution)/shard_map/prepare/pallas_call | solution.py:596
  8.1 35.7 %exchange_bulk.4 = (f32[16,128]{1,0:T(8,128)}, f32[4,16,128]{2,1,0:T(8,128)}, f32[16,128]{1,0:T(8,128)}, f32[16,128]{1,0:T(8,128)}, f32[4,2,384,128]{3,2,1,0:T(8,128)}) custom-call(f32[4,16,128]{2,1,0:T(8,128)} %bitcast.63, f32[16,128]{1,0:T(8,128)} %bitcast.85, f32[16,128]{1,0:T(8,128)} %bitcast.83, f32[16,128]{1,0:T(8,128)} %bitcast.84, f32[2,384,128]{2,1,0:T(8,128)} %refs_5_.1), custom_call_target="tpu_custom_call" | custom-call | tf_op jit(solution)/shard_map/exchange_bulk/pallas_call | solution.py:203
  43.8 6.9 %step.4 = (f32[2,384,128]{2,1,0:T(8,128)}, f32[2,64]{1,0:T(2,128)}, f32[2,384,128]{2,1,0:T(8,128)}, f32[2,64]{1,0:T(2,128)}, f32[4,2,8,128]{3,2,1,0:T(8,128)}, /...) custom-call(s32[3,8]{1,0:T(4,128)} %copy.19.refs_0_, f32[3]{0:T(128)} %pad_maximum_fusion.flags.refs_1_, ...), custom_call_target="tpu_custom_call" | custom-call | tf_op jit(solution)/shard_map/step/pallas_call | solution.py:618
  50.7 26.9 %exchange_bulk.5 = (f32[16,128]{1,0:T(8,128)}, f32[4,16,128]{2,1,0:T(8,128)}, f32[16,128]{1,0:T(8,128)}, f32[16,128]{1,0:T(8,128)}, f32[4,2,384,128]{3,2,1,0:T(8,128)}) custom-call(f32[4,16,128]{2,1,0:T(8,128)} %bitcast.62, f32[16,128]{1,0:T(8,128)} %bitcast.82, f32[16,128]{1,0:T(8,128)} %bitcast.80, f32[16,128]{1,0:T(8,128)} %bitcast.81, ...), custom_call_target="tpu_custom_call" | custom-call | tf_op jit(solution)/shard_map/exchange_bulk/pallas_call | solution.py:203
  77.6 7.2 %step.5 = (f32[2,384,128]{2,1,0:T(8,128)}, f32[2,64]{1,0:T(2,128)}, f32[2,8,128]{2,1,0:T(8,128)}, f32[4,2,8,128]{3,2,1,0:T(8,128)}, f32[2,384,128]{2,1,0:T(8,128...) custom-call(s32[3,8]{1,0:T(4,128)} %copy.19.refs_0_, ...), custom_call_target="tpu_custom_call" | custom-call | tf_op jit(solution)/shard_map/step/pallas_call | solution.py:618
  84.8 25.5 %exchange_bulk.6 = (f32[16,128]{1,0:T(8,128)}, f32[4,16,128]{2,1,0:T(8,128)}, f32[16,128]{1,0:T(8,128)}, f32[16,128]{1,0:T(8,128)}, f32[4,2,384,128]{3,2,1,0:T(8,128)}) custom-call(f32[4,16,128]{2,1,0:T(8,128)} %bitcast.60, f32[16,128]{1,0:T(8,128)} %bitcast.72, f32[16,128]{1,0:T(8,128)} %bitcast.70, f32[16,128]{1,0:T(8,128)} %bitcast.71, ...), custom_call_target="tpu_custom_call" | custom-call | tf_op jit(solution)/shard_map/exchange_bulk/pallas_call | solution.py:203
  110.3 7.8 %step.6 = (f32[2,384,128]{2,1,0:T(8,128)}, f32[2,64]{1,0:T(2,128)}, f32[2,8,128]{2,1,0:T(8,128)}, f32[4,2,8,128]{3,2,1,0:T(8,128)}, f32[2,384,128]{2,1,0:T(8,128...) custom-call(s32[3,8]{1,0:T(4,128)} %copy.19.refs_0_, ...), custom_call_target="tpu_custom_call" | custom-call | tf_op jit(solution)/shard_map/step/pallas_call | solution.py:618
  118.2 29.0 %exchange_bulk.7 = (f32[16,128]{1,0:T(8,128)}, f32[4,16,128]{2,1,0:T(8,128)}, f32[16,128]{1,0:T(8,128)}, f32[16,128]{1,0:T(8,128)}, f32[4,2,384,128]{3,2,1,0:T(8,128)}) custom-call(f32[4,16,128]{2,1,0:T(8,128)} %bitcast.61, f32[16,128]{1,0:T(8,128)} %bitcast.77, f32[16,128]{1,0:T(8,128)} %bitcast.75, f32[16,128]{1,0:T(8,128)} %bitcast.76, ...), custom_call_target="tpu_custom_call" | custom-call | tf_op jit(solution)/shard_map/exchange_bulk/pallas_call | solution.py:203
  147.1 7.2 %step.7 = (f32[2,384,128]{2,1,0:T(8,128)}, f32[2,64]{1,0:T(2,128)}, f32[2,8,128]{2,1,0:T(8,128)}, f32[4,2,8,128]{3,2,1,0:T(8,128)}, f32[2,384,128]{2,1,0:T(8,128...) custom-call(s32[3,8]{1,0:T(4,128)} %copy.19.refs_0_, ...), custom_call_target="tpu_custom_call" | custom-call | tf_op jit(solution)/shard_map/step/pallas_call | solution.py:618
  154.3 19.6 %exchange_sums.1.refs_4_ = f32[8,128]{1,0:T(8,128)} custom-call(f32[4,8,128]{2,1,0:T(8,128)} %bitcast.65), custom_call_target="tpu_custom_call" | custom-call | tf_op jit(solution)/shard_map/exchange_sums/pallas_call | solution.py:203
  173.9 3.4 %finish.1 = (f32[2,384,128]{2,1,0:T(8,128)}, f32[2,64]{1,0:T(2,128)}) custom-call(f32[2,8,128]{2,1,0:T(8,128)} %bitcast.44, f32[2,8,128]{2,1,0:T(8,128)} %bitcast.52, f32[2,8,128]{2,1,0:T(8,128)} %bitcast.55, f32[2,8,128]{2,1,0:T(8,128)} %bitcast.59, f32[8,128]{1,0:T(8,128)} %exchange_sums.1.refs_4_, f32[2,384,128]{2,1,0:T(8,128)} %refs_5_.1, ...), custom_call_target="tpu_custom_call" | custom-call | tf_op jit(solution)/shard_map/finish/pallas_call | solution.py:643
  (2 shorter events, 0.0 us)

commit v5 on v4

--- a/solution.py
+++ b/solution.py
@@ -48,7 +48,8 @@
     (x_slots, c_slots, z_slots, y_slots) = refs[:4]
     (x_send, x_recv, c_send, c_recv, z_send, z_recv, y_send, y_recv) = refs[4:12]
     if bulk:
-        (bulk_send, bulk_recv, side_send, side_recv, edge_send, edge_recv, own_sem) = refs[12:]
+        (bulk_send, bulk_recv, side_send, side_recv, edge_send, edge_recv, own_sem) = refs[12:19]
+        (cross_send, pass_send, pass_recv, c_land) = refs[19:]
     sec = lax.axis_index("sec")
     x = lax.axis_index("ch")
     c = lax.rem(sec, c_size)
@@ -75,8 +76,12 @@
     greeted = []
     for size, peer in ((x_size, x_peer), (c_size, c_peer), (z_size, z_peer), (y_size, y_peer)):
         greeted += [peer(d) for d in range(1, size)]
+    def cross_peer(d):
+        return dict(x_peer(d), **c_peer(1))
+
     if bulk:
         greeted += [up, down]
+        greeted += [cross_peer(d) for d in range(1, x_size)]
     barrier = pltpu.get_barrier_semaphore()
     for peer in greeted:
         pl.semaphore_signal(barrier, inc=1, device_id=peer, device_id_type=MESH)
@@ -131,9 +136,11 @@
             value = value + slots[k]
         return value
 
-    c_slots[c, 0:rows] = total(x_slots, x_size)
-    if bulk:
-        c_slots[c, rows:] = edge_in[...]
+    if bulk:
+        c_slots[0] = total(x_slots, x_size)
+        c_slots[1] = edge_in[...]
+    else:
+        c_slots[c] = total(x_slots, x_size)
 
     def stage(slots, me, size, peer, send, recv):
         copies = []
@@ -145,7 +152,11 @@
             copy.wait()
         return total(slots, size)
 
-    z_slots[z] = stage(c_slots, c, c_size, c_peer, c_send, c_recv)
+    if bulk:
+        remote(c_slots.at[1 - c], c_land, c_send.at[0], c_recv.at[0], c_peer(1)).wait()
+        z_slots[z] = c_slots[c] + c_land[...]
+    else:
+        z_slots[z] = stage(c_slots, c, c_size, c_peer, c_send, c_recv)
     y_slots[y] = stage(z_slots, z, z_size, z_peer, z_send, z_recv)
     if bulk:
         for copy in near:
@@ -155,22 +166,60 @@
                 held = full_out.at[lax.rem(x + x_size - d, x_size), half]
                 later.append(remote(held, held, bulk_send.at[sem], bulk_recv.at[sem], x_peer(d)))
     value = stage(y_slots, y, y_size, y_peer, y_send, y_recv)
-    sum_out[...] = value[0:rows]
-    if bulk:
-        edge_out[x] = value[rows:]
+    if not bulk:
+        sum_out[...] = value
+        return
+
+    def pass_sums():
+        return pltpu.make_async_remote_copy(
+            src_ref=sum_out,
+            dst_ref=sum_out,
+            send_sem=pass_send,
+            recv_sem=pass_recv,
+            device_id=c_peer(1),
+            device_id_type=MESH,
+        )
+
+    def edge_from(d):
+        place = edge_out.at[lax.rem(x + x_size - d, x_size)]
+        return pltpu.make_async_remote_copy(
+            src_ref=place,
+            dst_ref=place,
+            send_sem=edge_send.at[d],
+            recv_sem=edge_recv.at[d],
+            device_id=cross_peer(d),
+            device_id_type=MESH,
+        )
+
+    @pl.when(c == 0)
+    def _():
+        sum_out[...] = value
+        copy = pass_sums()
+        copy.start()
+        copy.wait_send()
+        for d in range(x_size):
+            edge_from(d).wait_recv()
+
+    @pl.when(c == 1)
+    def _():
+        edge_out[x] = value
+        place = edge_out.at[x]
         copies = []
-        for d in range(1, x_size):
-            copies.append(
-                remote(
-                    edge_out.at[x],
-                    edge_out.at[x],
-                    edge_send.at[d - 1],
-                    edge_recv.at[d - 1],
-                    x_peer(d),
-                )
-            )
-        for copy in copies + later:
+        across = []
+        for d in range(x_size):
+            across.append(
+                remote(place, place, cross_send.at[d], edge_recv.at[d], cross_peer(d))
+            )
+            if d:
+                copies.append(remote(place, place, edge_send.at[d], edge_recv.at[d], x_peer(d)))
+        for copy in across:
+            copy.wait_send()
+        for copy in copies:
             copy.wait()
+        pass_sums().wait_recv()
+
+    for copy in later:
+        copy.wait()
 
 
 def exchange(dims, ghosts, edges=None, first=None, last=None, outer=None):
@@ -186,7 +235,6 @@
     if bulk:
         args += [edges, first, last, outer]
         side = edges.shape
-        width = rows + side[0]
         outs += [shape((x_size,) + side), shape(side), shape(side), shape((x_size,) + outer.shape)]
     dma = pltpu.SemaphoreType.DMA
     scratch = [
@@ -199,7 +247,8 @@
         scratch += [dma((max(size - 1, 1),)), dma((max(size - 1, 1),))]
     if bulk:
         scratch += [dma((x_size,)), dma((x_size,)), dma((2,)), dma((2,))]
-        scratch += [dma((x_size - 1,)), dma((x_size - 1,)), dma]
+        scratch += [dma((x_size,)), dma((x_size,)), dma]
+        scratch += [dma((x_size,)), dma, dma, pltpu.VMEM((rows, lanes), jnp.float32)]
     return pl.pallas_call(
         functools.partial(exchange_kernel, dims, bulk),
         out_shape=outs,

time: 178 us -> 164 us (0.921)
  Pallas kernels: 172 us -> 158 us
    pallas_call x5, Pallas kernels: 137 us -> 123 us  [exchange(): pl.pallas_call(functools.partial(exchange_kernel, dims, bulk), out_shape=...]
where the time goes in v5:
time: 164 us; the launch traced here: 163 us
  Pallas kernels  158 us (96%)
  other arithmetic  2.8 us (2%)
  local copies, waits for them, and re-layouts  1.7 us (1%)
    pallas_call x5, Pallas kernels, exchange(): pl.pallas_call(functools.partial(exchange_kernel, dims, bulk), out_shape=...  123 us
    pallas_call x4, Pallas kernels, per_device(): pl.pallas_call(functools.partial(step_kernel, column, last_step), out_sha...  28.8 us
    pallas_call x1, Pallas kernels, per_device(): pl.pallas_call(functools.partial(finish_kernel, 2 * rows_dev), out_shape=...  3.42 us

profile of v5, /device:TPU:1, one launch (start us, length us, event | category | flops | bytes accessed | tf_op | source)
XLA Modules:
  0.0 163.0 jit_solution(14981403078438213821)
XLA Ops:
  0.6 0.6 pad_maximum_fusion.flags.refs_1_
  1.3 0.8 dynamic-slice_compare_fusion.1
  2.0 0.1 copy.16
  2.1 0.1 copy.17
  2.2 0.8 constant_dynamic-slice_fusion
  3.0 0.1 copy.18
  3.1 0.7 select_reduce_fusion
  3.8 0.6 copy.19.refs_0_
  4.5 0.7 select_select_fusion.refs_2_
  5.2 2.9 %prepare.1 = (f32[4,2,8,128]{3,2,1,0:T(8,128)}, f32[2,8,128]{2,1,0:T(8,128)}, f32[2,8,128]{2,1,0:T(8,128)}, f32[2,8,128]{2,1,0:T(8,128)}) custom-call(f32[3]{0:T(128)} %pad_maximum_fusion.flags.refs_1_, f32[2,384,128]{2,1,0:T(8,128)} %refs_5_.1, f32[2,64]{1,0:T(2,128)} %refs_9_.1, f32[2,64,1536]{2,1,0:T(8,128)} %refs_4_.9), custom_call_target="tpu_custom_call" | custom-call | tf_op jit(solution)/shard_map/prepare/pallas_call | solution.py:645
  8.1 34.3 %exchange_bulk.4 = (f32[16,128]{1,0:T(8,128)}, f32[4,16,128]{2,1,0:T(8,128)}, f32[16,128]{1,0:T(8,128)}, f32[16,128]{1,0:T(8,128)}, f32[4,2,384,128]{3,2,1,0:T(8,128)}) custom-call(f32[4,16,128]{2,1,0:T(8,128)} %bitcast.63, f32[16,128]{1,0:T(8,128)} %bitcast.85, f32[16,128]{1,0:T(8,128)} %bitcast.83, f32[16,128]{1,0:T(8,128)} %bitcast.84, f32[2,384,128]{2,1,0:T(8,128)} %refs_5_.1), custom_call_target="tpu_custom_call" | custom-call | tf_op jit(solution)/shard_map/exchange_bulk/pallas_call | solution.py:252
  42.4 6.9 %step.4 = (f32[2,384,128]{2,1,0:T(8,128)}, f32[2,64]{1,0:T(2,128)}, f32[2,384,128]{2,1,0:T(8,128)}, f32[2,64]{1,0:T(2,128)}, f32[4,2,8,128]{3,2,1,0:T(8,128)}, /...) custom-call(s32[3,8]{1,0:T(4,128)} %copy.19.refs_0_, f32[3]{0:T(128)} %pad_maximum_fusion.flags.refs_1_, ...), custom_call_target="tpu_custom_call" | custom-call | tf_op jit(solution)/shard_map/step/pallas_call | solution.py:667
  49.2 23.1 %exchange_bulk.5 = (f32[16,128]{1,0:T(8,128)}, f32[4,16,128]{2,1,0:T(8,128)}, f32[16,128]{1,0:T(8,128)}, f32[16,128]{1,0:T(8,128)}, f32[4,2,384,128]{3,2,1,0:T(8,128)}) custom-call(f32[4,16,128]{2,1,0:T(8,128)} %bitcast.62, f32[16,128]{1,0:T(8,128)} %bitcast.82, f32[16,128]{1,0:T(8,128)} %bitcast.80, f32[16,128]{1,0:T(8,128)} %bitcast.81, ...), custom_call_target="tpu_custom_call" | custom-call | tf_op jit(solution)/shard_map/exchange_bulk/pallas_call | solution.py:252
  72.4 7.2 %step.5 = (f32[2,384,128]{2,1,0:T(8,128)}, f32[2,64]{1,0:T(2,128)}, f32[2,8,128]{2,1,0:T(8,128)}, f32[4,2,8,128]{3,2,1,0:T(8,128)}, f32[2,384,128]{2,1,0:T(8,128...) custom-call(s32[3,8]{1,0:T(4,128)} %copy.19.refs_0_, ...), custom_call_target="tpu_custom_call" | custom-call | tf_op jit(solution)/shard_map/step/pallas_call | solution.py:667
  79.6 23.5 %exchange_bulk.6 = (f32[16,128]{1,0:T(8,128)}, f32[4,16,128]{2,1,0:T(8,128)}, f32[16,128]{1,0:T(8,128)}, f32[16,128]{1,0:T(8,128)}, f32[4,2,384,128]{3,2,1,0:T(8,128)}) custom-call(f32[4,16,128]{2,1,0:T(8,128)} %bitcast.60, f32[16,128]{1,0:T(8,128)} %bitcast.72, f32[16,128]{1,0:T(8,128)} %bitcast.70, f32[16,128]{1,0:T(8,128)} %bitcast.71, ...), custom_call_target="tpu_custom_call" | custom-call | tf_op jit(solution)/shard_map/exchange_bulk/pallas_call | solution.py:252
  103.1 7.6 %step.6 = (f32[2,384,128]{2,1,0:T(8,128)}, f32[2,64]{1,0:T(2,128)}, f32[2,8,128]{2,1,0:T(8,128)}, f32[4,2,8,128]{3,2,1,0:T(8,128)}, f32[2,384,128]{2,1,0:T(8,128...) custom-call(s32[3,8]{1,0:T(4,128)} %copy.19.refs_0_, ...), custom_call_target="tpu_custom_call" | custom-call | tf_op jit(solution)/shard_map/step/pallas_call | solution.py:667
  110.7 23.6 %exchange_bulk.7 = (f32[16,128]{1,0:T(8,128)}, f32[4,16,128]{2,1,0:T(8,128)}, f32[16,128]{1,0:T(8,128)}, f32[16,128]{1,0:T(8,128)}, f32[4,2,384,128]{3,2,1,0:T(8,128)}) custom-call(f32[4,16,128]{2,1,0:T(8,128)} %bitcast.61, f32[16,128]{1,0:T(8,128)} %bitcast.77, f32[16,128]{1,0:T(8,128)} %bitcast.75, f32[16,128]{1,0:T(8,128)} %bitcast.76, ...), custom_call_target="tpu_custom_call" | custom-call | tf_op jit(solution)/shard_map/exchange_bulk/pallas_call | solution.py:252
  134.3 7.2 %step.7 = (f32[2,384,128]{2,1,0:T(8,128)}, f32[2,64]{1,0:T(2,128)}, f32[2,8,128]{2,1,0:T(8,128)}, f32[4,2,8,128]{3,2,1,0:T(8,128)}, f32[2,384,128]{2,1,0:T(8,128...) custom-call(s32[3,8]{1,0:T(4,128)} %copy.19.refs_0_, ...), custom_call_target="tpu_custom_call" | custom-call | tf_op jit(solution)/shard_map/step/pallas_call | solution.py:667
  141.4 18.2 %exchange_sums.1.refs_4_ = f32[8,128]{1,0:T(8,128)} custom-call(f32[4,8,128]{2,1,0:T(8,128)} %bitcast.65), custom_call_target="tpu_custom_call" | custom-call | tf_op jit(solution)/shard_map/exchange_sums/pallas_call | solution.py:252
  159.6 3.4 %finish.1 = (f32[2,384,128]{2,1,0:T(8,128)}, f32[2,64]{1,0:T(2,128)}) custom-call(f32[2,8,128]{2,1,0:T(8,128)} %bitcast.44, f32[2,8,128]{2,1,0:T(8,128)} %bitcast.52, f32[2,8,128]{2,1,0:T(8,128)} %bitcast.55, f32[2,8,128]{2,1,0:T(8,128)} %bitcast.59, f32[8,128]{1,0:T(8,128)} %exchange_sums.1.refs_4_, f32[2,384,128]{2,1,0:T(8,128)} %refs_5_.1, ...), custom_call_target="tpu_custom_call" | custom-call | tf_op jit(solution)/shard_map/finish/pallas_call | solution.py:692
  (2 shorter events, 0.0 us)

commit v6 on v5

--- a/solution.py
+++ b/solution.py
@@ -144,7 +144,7 @@
 
     def stage(slots, me, size, peer, send, recv):
         copies = []
-        for d in range(1, size):
+        for d in sorted(range(1, size), key=lambda d: -min(d, size - d)):
             copies.append(
                 remote(slots.at[me], slots.at[me], send.at[d - 1], recv.at[d - 1], peer(d))
             )

time: 164 us -> 162 us (0.988)
  Pallas kernels: 158 us -> 156 us
where the time goes in v6:
time: 162 us
  Pallas kernels  156 us (96%)
  other arithmetic  2.8 us (2%)
  local copies, waits for them, and re-layouts  1.7 us (1%)
    pallas_call x5, Pallas kernels, exchange(): pl.pallas_call(functools.partial(exchange_kernel, dims, bulk), out_shape=...  121 us
    pallas_call x4, Pallas kernels, per_device(): pl.pallas_call(functools.partial(step_kernel, column, last_step), out_sha...  28.8 us
    pallas_call x1, Pallas kernels, per_device(): pl.pallas_call(functools.partial(finish_kernel, 2 * rows_dev), out_shape=...  3.42 us

profile of v6, /device:TPU:1, one launch (start us, length us, event | category | flops | bytes accessed | tf_op | source)
XLA Modules:
  0.0 161.6 jit_solution(1773471359140873286)
XLA Ops:
  0.6 0.6 pad_maximum_fusion.flags.refs_1_
  1.3 0.8 dynamic-slice_compare_fusion.1
  2.0 0.1 copy.16
  2.1 0.1 copy.17
  2.2 0.8 constant_dynamic-slice_fusion
  3.0 0.1 copy.18
  3.1 0.7 select_reduce_fusion
  3.8 0.6 copy.19.refs_0_
  4.5 0.7 select_select_fusion.refs_2_
  5.2 2.9 %prepare.1 = (f32[4,2,8,128]{3,2,1,0:T(8,128)}, f32[2,8,128]{2,1,0:T(8,128)}, f32[2,8,128]{2,1,0:T(8,128)}, f32[2,8,128]{2,1,0:T(8,128)}) custom-call(f32[3]{0:T(128)} %pad_maximum_fusion.flags.refs_1_, f32[2,384,128]{2,1,0:T(8,128)} %refs_5_.1, f32[2,64]{1,0:T(2,128)} %refs_9_.1, f32[2,64,1536]{2,1,0:T(8,128)} %refs_4_.9), custom_call_target="tpu_custom_call" | custom-call | tf_op jit(solution)/shard_map/prepare/pallas_call | solution.py:645
  8.1 33.7 %exchange_bulk.4 = (f32[16,128]{1,0:T(8,128)}, f32[4,16,128]{2,1,0:T(8,128)}, f32[16,128]{1,0:T(8,128)}, f32[16,128]{1,0:T(8,128)}, f32[4,2,384,128]{3,2,1,0:T(8,128)}) custom-call(f32[4,16,128]{2,1,0:T(8,128)} %bitcast.63, f32[16,128]{1,0:T(8,128)} %bitcast.85, f32[16,128]{1,0:T(8,128)} %bitcast.83, f32[16,128]{1,0:T(8,128)} %bitcast.84, f32[2,384,128]{2,1,0:T(8,128)} %refs_5_.1), custom_call_target="tpu_custom_call" | custom-call | tf_op jit(solution)/shard_map/exchange_bulk/pallas_call | solution.py:252
  41.8 6.9 %step.4 = (f32[2,384,128]{2,1,0:T(8,128)}, f32[2,64]{1,0:T(2,128)}, f32[2,384,128]{2,1,0:T(8,128)}, f32[2,64]{1,0:T(2,128)}, f32[4,2,8,128]{3,2,1,0:T(8,128)}, /...) custom-call(s32[3,8]{1,0:T(4,128)} %copy.19.refs_0_, f32[3]{0:T(128)} %pad_maximum_fusion.flags.refs_1_, ...), custom_call_target="tpu_custom_call" | custom-call | tf_op jit(solution)/shard_map/step/pallas_call | solution.py:667
  48.7 23.4 %exchange_bulk.5 = (f32[16,128]{1,0:T(8,128)}, f32[4,16,128]{2,1,0:T(8,128)}, f32[16,128]{1,0:T(8,128)}, f32[16,128]{1,0:T(8,128)}, f32[4,2,384,128]{3,2,1,0:T(8,128)}) custom-call(f32[4,16,128]{2,1,0:T(8,128)} %bitcast.62, f32[16,128]{1,0:T(8,128)} %bitcast.82, f32[16,128]{1,0:T(8,128)} %bitcast.80, f32[16,128]{1,0:T(8,128)} %bitcast.81, ...), custom_call_target="tpu_custom_call" | custom-call | tf_op jit(solution)/shard_map/exchange_bulk/pallas_call | solution.py:252
  72.1 7.2 %step.5 = (f32[2,384,128]{2,1,0:T(8,128)}, f32[2,64]{1,0:T(2,128)}, f32[2,8,128]{2,1,0:T(8,128)}, f32[4,2,8,128]{3,2,1,0:T(8,128)}, f32[2,384,128]{2,1,0:T(8,128...) custom-call(s32[3,8]{1,0:T(4,128)} %copy.19.refs_0_, ...), custom_call_target="tpu_custom_call" | custom-call | tf_op jit(solution)/shard_map/step/pallas_call | solution.py:667
  79.3 23.0 %exchange_bulk.6 = (f32[16,128]{1,0:T(8,128)}, f32[4,16,128]{2,1,0:T(8,128)}, f32[16,128]{1,0:T(8,128)}, f32[16,128]{1,0:T(8,128)}, f32[4,2,384,128]{3,2,1,0:T(8,128)}) custom-call(f32[4,16,128]{2,1,0:T(8,128)} %bitcast.60, f32[16,128]{1,0:T(8,128)} %bitcast.72, f32[16,128]{1,0:T(8,128)} %bitcast.70, f32[16,128]{1,0:T(8,128)} %bitcast.71, ...), custom_call_target="tpu_custom_call" | custom-call | tf_op jit(solution)/shard_map/exchange_bulk/pallas_call | solution.py:252
  102.3 7.6 %step.6 = (f32[2,384,128]{2,1,0:T(8,128)}, f32[2,64]{1,0:T(2,128)}, f32[2,8,128]{2,1,0:T(8,128)}, f32[4,2,8,128]{3,2,1,0:T(8,128)}, f32[2,384,128]{2,1,0:T(8,128...) custom-call(s32[3,8]{1,0:T(4,128)} %copy.19.refs_0_, ...), custom_call_target="tpu_custom_call" | custom-call | tf_op jit(solution)/shard_map/step/pallas_call | solution.py:667
  110.0 23.0 %exchange_bulk.7 = (f32[16,128]{1,0:T(8,128)}, f32[4,16,128]{2,1,0:T(8,128)}, f32[16,128]{1,0:T(8,128)}, f32[16,128]{1,0:T(8,128)}, f32[4,2,384,128]{3,2,1,0:T(8,128)}) custom-call(f32[4,16,128]{2,1,0:T(8,128)} %bitcast.61, f32[16,128]{1,0:T(8,128)} %bitcast.77, f32[16,128]{1,0:T(8,128)} %bitcast.75, f32[16,128]{1,0:T(8,128)} %bitcast.76, ...), custom_call_target="tpu_custom_call" | custom-call | tf_op jit(solution)/shard_map/exchange_bulk/pallas_call | solution.py:252
  133.0 7.2 %step.7 = (f32[2,384,128]{2,1,0:T(8,128)}, f32[2,64]{1,0:T(2,128)}, f32[2,8,128]{2,1,0:T(8,128)}, f32[4,2,8,128]{3,2,1,0:T(8,128)}, f32[2,384,128]{2,1,0:T(8,128...) custom-call(s32[3,8]{1,0:T(4,128)} %copy.19.refs_0_, ...), custom_call_target="tpu_custom_call" | custom-call | tf_op jit(solution)/shard_map/step/pallas_call | solution.py:667
  140.1 18.1 %exchange_sums.1.refs_4_ = f32[8,128]{1,0:T(8,128)} custom-call(f32[4,8,128]{2,1,0:T(8,128)} %bitcast.65), custom_call_target="tpu_custom_call" | custom-call | tf_op jit(solution)/shard_map/exchange_sums/pallas_call | solution.py:252
  158.2 3.4 %finish.1 = (f32[2,384,128]{2,1,0:T(8,128)}, f32[2,64]{1,0:T(2,128)}) custom-call(f32[2,8,128]{2,1,0:T(8,128)} %bitcast.44, f32[2,8,128]{2,1,0:T(8,128)} %bitcast.52, f32[2,8,128]{2,1,0:T(8,128)} %bitcast.55, f32[2,8,128]{2,1,0:T(8,128)} %bitcast.59, f32[8,128]{1,0:T(8,128)} %exchange_sums.1.refs_4_, f32[2,384,128]{2,1,0:T(8,128)} %refs_5_.1, ...), custom_call_target="tpu_custom_call" | custom-call | tf_op jit(solution)/shard_map/finish/pallas_call | solution.py:692
  (2 shorter events, 0.0 us)
